TPU v7x, 32 devices: a whole 2x2x4 slice. The times are simulated.
32 devices in a mesh: theta: 8 (over z, core), band: 4 (over y, x).
Axes of the slice: x: 2, y: 2, z: 4, core: 2. Of those that a mesh axis runs over, the one named last changes fastest.
Arguments:
- basis: float32 [4, 5, 4, 1024], P(None, None, 'band', 'theta'), may hold values from -8 to 8
- jac_block: float32 [5, 5, 4, 1024], P(None, None, 'band', 'theta'), may hold values from -3 to 3
- face_coef: float32 [4, 5, 4, 1024], P(None, None, 'band', 'theta'), may hold values from 0.1 to 1.1
- panel_inverse: bfloat16 [4, 16, 320, 640], P('band', 'theta'), may hold values from -0.2 to 1.2
- rotor_offset: int32 [1], replicated, may hold values from 448 to 575
Outputs:
- precond: float32 [5, 4, 1024], P(None, 'band', 'theta')
- v_next: float32 [5, 4, 1024], P(None, 'band', 'theta')
- hess: float32 [5], replicated
All inputs are finite; a program needn't handle non-finite values.
Results may differ from a plain program's by a relative error of at most 0.0029.
Values may be sent and summed in bfloat16 or wider, within the bound.
No kernel may reach another device: no remote copies, remote signals or barrier semaphores. Data moves between devices by JAX's collectives and lax.ppermute only.
A program may use at most 64 MiB of HBM per device.

v0:
```python
import jax
import jax.numpy as jnp
from jax import lax
from jax.sharding import PartitionSpec as P


def extended_2(x, sides, width):
    for axis, dim in sides:
        devices, length = (lax.axis_size(axis), x.shape[dim])
        up = [(i, (i + 1) % devices) for i in range(devices)]
        down = [(j, i) for i, j in up]
        last = lax.slice_in_dim(x, length - width, length, axis=dim)
        first = lax.slice_in_dim(x, 0, width, axis=dim)
        before = lax.ppermute(last, axis, up)
        after = lax.ppermute(first, axis, down)
        x = jnp.concatenate([before, x, after], axis=dim)
    return x


def on_device(basis, jac_block, face_coef, panel_inverse, rotor_offset):
    ncomp = basis.shape[1]
    rows_here = basis.shape[2]
    width = basis.shape[3]
    half_width = width // 2
    theta_count = lax.axis_size("theta")
    band_count = lax.axis_size("band")
    cycle_cells = width * theta_count
    total = ncomp * rows_here * band_count * cycle_cells
    theta_idx = lax.axis_index("theta")
    band_idx = lax.axis_index("band")
    resid16 = basis[-1].astype(jnp.bfloat16)
    extended = extended_2(resid16, (("theta", 2),), half_width)
    panels = (
        extended.reshape(ncomp, rows_here, 2, width)
        .transpose(1, 2, 0, 3)
        .reshape(rows_here, 2, ncomp * width)
    )
    owned = jnp.einsum("bpij,bpj->bpi", panel_inverse, panels, preferred_element_type=jnp.float32)
    precond = (
        owned.reshape(rows_here, 2, ncomp, half_width)
        .transpose(2, 0, 1, 3)
        .reshape(ncomp, rows_here, width)
    )
    padded = extended_2(precond, (("band", 1), ("theta", 2)), 1)
    low_row = padded[:, 0, 1:-1]
    up_row = padded[:, -1, 1:-1]
    offset = rotor_offset[0]
    up_start = (theta_idx * width + offset) % cycle_cells
    low_start = (theta_idx * width + cycle_cells - offset) % cycle_cells
    up_full, low_full = (
        lax.all_gather(up_row, "theta", axis=1, tiled=True),
        lax.all_gather(low_row, "theta", axis=1, tiled=True),
    )
    up_twice = jnp.concatenate([up_full, up_full], axis=1)
    low_twice = jnp.concatenate([low_full, low_full], axis=1)
    up_shift = lax.dynamic_slice_in_dim(up_twice, up_start, width, 1)
    low_shift = lax.dynamic_slice_in_dim(low_twice, low_start, width, 1)
    middle = band_count // 2
    zero_line = jnp.zeros_like(low_row)
    lower_first = jnp.where(
        band_idx == 0, zero_line, jnp.where(band_idx == middle, low_shift, low_row)
    )
    upper_last = jnp.where(
        band_idx == band_count - 1, zero_line, jnp.where(band_idx == middle - 1, up_shift, up_row)
    )
    inner = padded[:, :, 1:-1]
    band_minus = jnp.concatenate([lower_first[:, None], inner[:, 1:rows_here]], axis=1)
    band_plus = jnp.concatenate([inner[:, 2 : rows_here + 1], upper_last[:, None]], axis=1)
    theta_minus = padded[:, 1:-1, :width]
    theta_plus = padded[:, 1:-1, 2:]
    image = 6.0 * precond + jnp.sum(jac_block * precond[None], axis=1)
    image = image - (
        face_coef[0] * theta_minus
        + face_coef[1] * theta_plus
        + face_coef[2] * band_minus
        + face_coef[3] * band_plus
    )
    local_proj = jnp.sum(basis * image[None], axis=(1, 2, 3))
    local_gram = jnp.einsum("kabc,labc->kl", basis, basis, precision=lax.Precision.HIGHEST)
    summed, image_squares, gram = lax.psum(
        (local_proj, jnp.sum(image * image), local_gram), ("theta", "band")
    )
    proj = summed / total
    gram = gram / total
    ortho = image - jnp.sum(proj[:, None, None, None] * basis, axis=0)
    squares = (
        image_squares / total
        - 2.0 * jnp.sum(proj * proj)
        + jnp.sum(proj[:, None] * gram * proj[None, :])
    )
    hnorm = jnp.sqrt(squares + 1e-06)
    v_next = ortho / hnorm
    hess = jnp.concatenate([proj, hnorm[None]])
    return (precond, v_next, hess)


def solution(mesh):
    return jax.shard_map(
        on_device,
        mesh=mesh,
        in_specs=(
            P(None, None, "band", "theta"),
            P(None, None, "band", "theta"),
            P(None, None, "band", "theta"),
            P("band", "theta", None, None),
            P(),
        ),
        out_specs=(P(None, "band", "theta"), P(None, "band", "theta"), P()),
        check_vma=False,
    )
```

profile of v0, /device:TPU:0, one launch (start us, length us, event | category | flops | bytes accessed | tf_op | source)
XLA Modules:
  0.0 90.3 jit_solution(473157668063415873)
XLA Ops:
  0.6 0.0 copy-start
  0.6 0.8 slice.57
  1.4 0.1 fusion.20
  1.5 0.5 collective-permute-start
  2.0 4.1 %collective-permute-start.1 = (bf16[5,1,64]{2,0,1:T(8,128)(2,1)S(1)}, bf16[5,1,64]{2,0,1:T(8,128)(2,1)S(1)}, u32[]{:S(2)}, u32[]{:S(2)}) collective-permute-start(bf16[5,1,64]{2,0,1:T(8,128)(2,1)S(1)} %get-tuple-element.13), channel_id=1, source_target_pairs={{4,0},{8,4},{12,8},{16,12},{20,16},{24,20},{28,24},{0,28},{5,1},{9... | collective-permute-start | bytes 1928 | tf_op jit(solution)/shard_map/ppermute | solution.py:15
  6.7 0.0 copy-start.1
  6.7 0.7 copy-done.1
  7.4 0.0 copy-start.4
  7.4 0.1 convolution_bitcast_fusion
  7.6 0.6 copy-done.4
  8.1 0.0 collective-permute-done
  8.1 0.0 collective-permute-done.1
  8.1 0.1 pad_maximum_fusion.1
  8.2 0.0 copy-done
  8.2 0.3 fusion
  8.6 0.1 reshape.82
  8.7 0.1 reshape.83
  8.7 0.0 copy-start.2
  8.8 0.0 copy-start.3
  8.8 2.0 %collective-permute-start.2 = (f32[5,1,128]{2,0,1:T(8,128)S(1)}, f32[5,1,128]{2,0,1:T(8,128)S(1)}, u32[]{:S(2)}, u32[]{:S(2)}) collective-permute-start(f32[5,1,128]{2,0,1:T(8,128)S(1)} %copy.29), channel_id=1, source_target_pairs={{0,1},{1,2},{2,3},{3,0},{4,5},{5,6},{6,7},{7,4},{8,9},{9,10},{10,1... | collective-permute-start | bytes 7688 | tf_op jit(solution)/shard_map/ppermute | solution.py:14
  10.8 1.0 %collective-permute-start.3 = (f32[5,1,128]{2,0,1:T(8,128)S(1)}, f32[5,1,128]{2,0,1:T(8,128)S(1)}, u32[]{:S(2)}, u32[]{:S(2)}) collective-permute-start(f32[5,1,128]{2,0,1:T(8,128)S(1)} %copy.29), channel_id=1, source_target_pairs={{1,0},{2,1},{3,2},{0,3},{5,4},{6,5},{7,6},{4,7},{9,8},{10,9},{11,1... | collective-permute-start | bytes 7688 | tf_op jit(solution)/shard_map/ppermute | solution.py:15
  11.8 0.1 mul.92
  11.9 0.0 copy-done.3
  11.9 1.4 %collective-permute-done.2 = f32[5,1,128]{2,0,1:T(8,128)S(1)} collective-permute-done((f32[5,1,128]{2,0,1:T(8,128)S(1)}, f32[5,1,128]{2,0,1:T(8,128)S(1)}, u32[]{:S(2)}, u32[]{:S(2)}) %collective-permute-start.2) | collective-permute-done | bytes 2592 | tf_op jit(solution)/shard_map/ppermute | solution.py:14
  13.3 1.0 %collective-permute-done.3 = f32[5,1,128]{2,0,1:T(8,128)S(1)} collective-permute-done((f32[5,1,128]{2,0,1:T(8,128)S(1)}, f32[5,1,128]{2,0,1:T(8,128)S(1)}, u32[]{:S(2)}, u32[]{:S(2)}) %collective-permute-start.3) | collective-permute-done | bytes 2592 | tf_op jit(solution)/shard_map/ppermute | solution.py:15
  14.4 0.1 fusion.18
  14.5 0.0 collective-permute-start.4
  14.5 3.5 %collective-permute-start.5 = (f32[5,3,1]{2,1,0:T(4,128)S(1)}, f32[5,3,1]{2,1,0:T(4,128)S(1)}, u32[]{:S(2)}, u32[]{:S(2)}) collective-permute-start(f32[5,3,1]{2,1,0:T(4,128)S(1)} %get-tuple-element.9), channel_id=1, source_target_pairs={{4,0},{8,4},{12,8},{16,12},{20,16},{24,20},{28,24},{0,28},{5,1},{9... | collective-permute-start | bytes 188 | tf_op jit(solution)/shard_map/ppermute | solution.py:15
  18.0 14.1 %all-gather = f32[5,1,1024]{2,0,1:T(8,128)S(1)} all-gather(f32[5,1,128]{2,0,1:T(8,128)S(1)} %collective-permute-done.2), channel_id=2, replica_groups=mesh['theta'=8,'band'=4] {'theta'}, dimensions={2}, use_global_device_ids=true | all-gather | bytes 23040 | tf_op jit(solution)/shard_map/all_gather | solution.py:52
  32.1 14.1 %all-gather.1 = f32[5,1,1024]{2,0,1:T(8,128)S(1)} all-gather(f32[5,1,128]{2,0,1:T(8,128)S(1)} %collective-permute-done.3), channel_id=3, replica_groups=mesh['theta'=8,'band'=4] {'theta'}, dimensions={2}, use_global_device_ids=true | all-gather | bytes 23040 | tf_op jit(solution)/shard_map/all_gather | solution.py:51
  46.2 0.1 fusion.11
  46.2 0.1 fusion.9
  46.3 0.0 collective-permute-done.4
  46.3 0.0 collective-permute-done.5
  46.3 0.0 copy-done.2
  46.3 0.7 multiply_reduce_fusion.3
  47.1 0.1 multiply_reduce_fusion.2
  47.2 38.4 %all-reduce = (f32[4]{0:T(128)S(1)}, f32[]{:T(128)}, f32[4,4]{1,0:T(4,128)S(1)}) all-reduce(f32[4]{0:T(128)S(1)} %multiply_reduce_fusion.2, f32[]{:T(128)} %get-tuple-element.6, f32[4,4]{1,0:T(4,128)S(1)} %convolution_bitcast_fusion), channel_id=1, replica_groups=mesh['theta'=8,'band'=4] {'theta','band'}, use_global_device_ids=true, to_apply=%region_2.3 | all-reduce | flops 21 | bytes 168 | tf_op jit(solution)/shard_map/psum | solution.py:80
  85.6 0.6 broadcast_multiply_fusion
  86.2 0.1 multiply_reduce_fusion.1
  86.3 0.7 multiply_reduce_fusion.4
  89.1 0.6 pad_maximum_fusion.8
  89.7 0.6 subtract_divide_fusion
  (12 shorter events, 0.1 us)
Async XLA Ops:
  0.6 7.6 %copy-start = (bf16[1,2,320,640]{3,2,1,0:T(8,128)(2,1)S(1)}, bf16[1,2,320,640]{3,2,1,0:T(8,128)(2,1)}, u32[]{:S(2)}) copy-start(bf16[1,2,320,640]{3,2,1,0:T(8,128)(2,1)} %param.8) | copy-start | bytes 2457604
  1.5 6.6 %collective-permute-start = (bf16[5,1,64]{2,0,1:T(8,128)(2,1)S(1)}, bf16[5,1,64]{2,0,1:T(8,128)(2,1)S(1)}, u32[]{:S(2)}, u32[]{:S(2)}) collective-permute-start(bf16[5,1,64]{2,0,1:T(8,128)(2,1)S(1)} %get-tuple-element.12), channel_id=1, source_target_pairs={{0,4},{4,8},{8,12},{12,16},{16,20},{20,24},{24,28},{28,0},{1,5},{5... | collective-permute-start | bytes 1928 | tf_op jit(solution)/shard_map/ppermute | solution.py:14
  2.0 6.2 %collective-permute-start.1 = (bf16[5,1,64]{2,0,1:T(8,128)(2,1)S(1)}, bf16[5,1,64]{2,0,1:T(8,128)(2,1)S(1)}, u32[]{:S(2)}, u32[]{:S(2)}) collective-permute-start(bf16[5,1,64]{2,0,1:T(8,128)(2,1)S(1)} %get-tuple-element.13), channel_id=1, source_target_pairs={{4,0},{8,4},{12,8},{16,12},{20,16},{24,20},{28,24},{0,28},{5,1},{9... | collective-permute-start | bytes 1928 | tf_op jit(solution)/shard_map/ppermute | solution.py:15
  6.7 0.7 copy-start.1
  7.4 0.7 copy-start.4
  8.7 37.6 %copy-start.2 = (f32[5,1,128]{2,1,0:T(1,128)}, f32[5,1,128]{2,1,0:T(1,128)S(1)}, u32[]{:S(2)}) copy-start(f32[5,1,128]{2,1,0:T(1,128)S(1)} %reshape.83) | copy-start | bytes 7684
  8.8 3.1 %copy-start.3 = (f32[5,5,1,128]{3,2,1,0:T(1,128)S(1)}, f32[5,5,1,128]{3,2,1,0:T(1,128)}, u32[]{:S(2)}) copy-start(f32[5,5,1,128]{3,2,1,0:T(1,128)} %param.6) | copy-start | bytes 38404
  8.8 4.6 %collective-permute-start.2 = (f32[5,1,128]{2,0,1:T(8,128)S(1)}, f32[5,1,128]{2,0,1:T(8,128)S(1)}, u32[]{:S(2)}, u32[]{:S(2)}) collective-permute-start(f32[5,1,128]{2,0,1:T(8,128)S(1)} %copy.29), channel_id=1, source_target_pairs={{0,1},{1,2},{2,3},{3,0},{4,5},{5,6},{6,7},{7,4},{8,9},{9,10},{10,1... | collective-permute-start | bytes 7688 | tf_op jit(solution)/shard_map/ppermute | solution.py:14
  10.8 3.6 %collective-permute-start.3 = (f32[5,1,128]{2,0,1:T(8,128)S(1)}, f32[5,1,128]{2,0,1:T(8,128)S(1)}, u32[]{:S(2)}, u32[]{:S(2)}) collective-permute-start(f32[5,1,128]{2,0,1:T(8,128)S(1)} %copy.29), channel_id=1, source_target_pairs={{1,0},{2,1},{3,2},{0,3},{5,4},{6,5},{7,6},{4,7},{9,8},{10,9},{11,1... | collective-permute-start | bytes 7688 | tf_op jit(solution)/shard_map/ppermute | solution.py:15
  14.5 31.9 %collective-permute-start.4 = (f32[5,3,1]{2,1,0:T(4,128)S(1)}, f32[5,3,1]{2,1,0:T(4,128)S(1)}, u32[]{:S(2)}, u32[]{:S(2)}) collective-permute-start(f32[5,3,1]{2,1,0:T(4,128)S(1)} %get-tuple-element.8), channel_id=1, source_target_pairs={{0,4},{4,8},{8,12},{12,16},{16,20},{20,24},{24,28},{28,0},{1,5},{5... | collective-permute-start | bytes 188 | tf_op jit(solution)/shard_map/ppermute | solution.py:14
  14.5 31.9 %collective-permute-start.5 = (f32[5,3,1]{2,1,0:T(4,128)S(1)}, f32[5,3,1]{2,1,0:T(4,128)S(1)}, u32[]{:S(2)}, u32[]{:S(2)}) collective-permute-start(f32[5,3,1]{2,1,0:T(4,128)S(1)} %get-tuple-element.9), channel_id=1, source_target_pairs={{4,0},{8,4},{12,8},{16,12},{20,16},{24,20},{28,24},{0,28},{5,1},{9... | collective-permute-start | bytes 188 | tf_op jit(solution)/shard_map/ppermute | solution.py:15
where the time goes:
time: 91.1 us; the launch traced here: 90.3 us
  blocking collectives  66.6 us (73%)
  starting transfers between devices  11.1 us (12%)
  other arithmetic  3.72 us (4%)
  between operations  3.42 us (4%)
  waiting for transfers between devices  2.48 us (3%)
  local copies, waits for them, and re-layouts  2.47 us (3%)
    psum x1, blocking collectives, on_device(): lax.psum((local_proj, jnp.sum(image * image), local_gram), ('theta', 'ban...  38.4 us
    all_gather x1, blocking collectives, on_device(): lax.all_gather(low_row, 'theta', axis=1, tiled=True)  14.1 us
    all_gather x1, blocking collectives, on_device(): lax.all_gather(up_row, 'theta', axis=1, tiled=True)  14.1 us
    ppermute x3, starting transfers between devices, extended_2(): after = lax.ppermute(first, axis, down)  8.63 us
    ppermute x3, starting transfers between devices, extended_2(): before = lax.ppermute(last, axis, up)  2.5 us
  transfers between devices with their start and end apart: 6, of which 2 were waited for; matrix products, arithmetic and copies ran while one was open for 0% of the time, Pallas kernels for 0%

commit v1 on v0

v1 whole, which is shorter than its diff:
```python
import jax
import jax.numpy as jnp
from jax import lax
from jax.experimental import pallas as pl
from jax.experimental.pallas import tpu as pltpu
from jax.sharding import PartitionSpec as P

AXES = ("theta", "band")


def lane_reduced(rows):
    count, width = rows.shape
    sums = jnp.sum(rows, axis=1, keepdims=True)
    row = lax.broadcasted_iota(jnp.int32, (count, width), 0)
    lane = lax.broadcasted_iota(jnp.int32, (count, width), 1)
    return jnp.sum(jnp.where(row == lane, sums, 0.0), axis=0, keepdims=True)


def image_kernel(theta_count, band_count, offset_ref, all_ref, basis_ref, jac_ref, face_ref, image_ref, send_ref):
    kb, ncomp, _, width = basis_ref.shape
    cycle = theta_count * width
    middle = band_count // 2
    theta = lax.axis_index("theta")
    band = lax.axis_index("band")
    offset = offset_ref[0]

    def cells_of(t, b):
        t = jnp.where(t >= theta_count, t - theta_count, t)
        return all_ref[t * band_count + b].reshape(ncomp, width)

    lane = lax.broadcasted_iota(jnp.int32, (ncomp, width), 1)

    def shifted(row, shift):
        start = theta * width + shift
        first = lax.rem(start // width, theta_count)
        skip = lax.rem(start, width)
        back = lax.rem(width - skip, width)
        one = pltpu.roll(cells_of(first, row), back, 1)
        two = pltpu.roll(cells_of(first + 1, row), back, 1)
        return jnp.where(lane < width - skip, one, two)

    precond = cells_of(theta, band)
    before = cells_of(theta + theta_count - 1, band)
    after = cells_of(theta + 1, band)
    theta_minus = jnp.where(lane == 0, pltpu.roll(before, 1, 1), pltpu.roll(precond, 1, 1))
    theta_plus = jnp.where(lane == width - 1, pltpu.roll(after, width - 1, 1), pltpu.roll(precond, width - 1, 1))
    up_shift = jnp.where(band == middle - 1, offset, 0)
    low_shift = jnp.where(band == middle, cycle - offset, 0)
    band_plus = shifted(jnp.minimum(band + 1, band_count - 1), up_shift)
    band_plus = jnp.where(band == band_count - 1, 0.0, band_plus)
    band_minus = shifted(jnp.maximum(band - 1, 0), low_shift)
    band_minus = jnp.where(band == 0, 0.0, band_minus)

    coupled = jac_ref[:, 0, 0, :] * precond[0:1]
    for w in range(1, ncomp):
        coupled += jac_ref[:, w, 0, :] * precond[w : w + 1]
    image = 6.0 * precond + coupled
    image = image - (
        face_ref[0, :, 0, :] * theta_minus
        + face_ref[1, :, 0, :] * theta_plus
        + face_ref[2, :, 0, :] * band_minus
        + face_ref[3, :, 0, :] * band_plus
    )
    image_ref[...] = image
    vectors = [basis_ref[i, :, 0, :] for i in range(kb)]
    pairs = [vectors[i] * image for i in range(kb)] + [image * image]
    pairs += [vectors[i] * vectors[j] for i in range(kb) for j in range(kb)]
    rows = jnp.concatenate([jnp.sum(pair, axis=0, keepdims=True) for pair in pairs], axis=0)
    send_ref[...] = jnp.broadcast_to(lane_reduced(rows), send_ref.shape)


def finish_kernel(total, sums_ref, image_ref, basis_ref, next_ref, hess_ref):
    kb = basis_ref.shape[0]
    sums = jnp.sum(sums_ref[...], axis=0, keepdims=True) / total
    proj = [sums[0, i] for i in range(kb)]
    squares = sums[0, kb]
    for i in range(kb):
        squares -= 2.0 * proj[i] * proj[i]
    for i in range(kb):
        for j in range(kb):
            squares += proj[i] * sums[0, kb + 1 + i * kb + j] * proj[j]
    ortho = image_ref[...]
    drop = proj[0] * basis_ref[0, :, 0, :]
    for i in range(1, kb):
        drop += proj[i] * basis_ref[i, :, 0, :]
    ortho = ortho - drop
    hnorm = jnp.sqrt(jnp.full(sums.shape, squares + 1e-06, jnp.float32))
    next_ref[:, 0, :] = ortho / hnorm
    lane = lax.broadcasted_iota(jnp.int32, sums.shape, 1)
    hess_ref[...] = jnp.where(lane < kb, sums, hnorm)[:, : kb + 1]


def on_device(basis, jac_block, face_coef, panel_inverse, rotor_offset):
    kb, ncomp, rows_here, width = basis.shape
    assert rows_here == 1
    half = width // 2
    theta_count = lax.axis_size("theta")
    band_count = lax.axis_size("band")
    devices = theta_count * band_count
    total = ncomp * devices * width
    up = [(i, (i + 1) % theta_count) for i in range(theta_count)]
    down = [(j, i) for i, j in up]
    before = lax.ppermute(basis, "theta", up)[-1].astype(jnp.bfloat16)
    after = lax.ppermute(basis, "theta", down)[-1].astype(jnp.bfloat16)
    current = basis[-1].astype(jnp.bfloat16)
    extended = jnp.concatenate([before[..., half:], current, after[..., :half]], axis=2)
    panels = extended.reshape(ncomp, 2, width).transpose(1, 0, 2).reshape(2, ncomp * width)
    owned = jnp.einsum("pij,pj->pi", panel_inverse[0], panels, preferred_element_type=jnp.float32)
    precond = owned.reshape(2, ncomp, half).transpose(1, 0, 2).reshape(ncomp, 1, width)

    copies = jnp.broadcast_to(precond[None], (devices, ncomp, 1, width))
    everyone = lax.all_to_all(copies, AXES, 0, 0, tiled=True)

    smem = pl.BlockSpec(memory_space=pltpu.SMEM)
    vmem = pl.BlockSpec(memory_space=pltpu.VMEM)
    image, partial = pl.pallas_call(
        lambda *refs: image_kernel(theta_count, band_count, *refs),
        out_shape=(
            jax.ShapeDtypeStruct((ncomp, width), jnp.float32),
            jax.ShapeDtypeStruct((devices, width), jnp.float32),
        ),
        in_specs=[smem, vmem, vmem, vmem, vmem],
        out_specs=(vmem, vmem),
        name="image",
    )(rotor_offset, everyone, basis, jac_block, face_coef)
    sums = lax.all_to_all(partial, AXES, 0, 0, tiled=True)
    v_next, hess = pl.pallas_call(
        lambda *refs: finish_kernel(total, *refs),
        out_shape=(
            jax.ShapeDtypeStruct((ncomp, 1, width), jnp.float32),
            jax.ShapeDtypeStruct((1, kb + 1), jnp.float32),
        ),
        in_specs=[vmem, vmem, vmem],
        out_specs=(vmem, vmem),
        name="finish",
    )(sums, image, basis)
    return precond, v_next, hess.reshape(kb + 1)


def solution(mesh):
    return jax.shard_map(
        on_device,
        mesh=mesh,
        in_specs=(
            P(None, None, "band", "theta"),
            P(None, None, "band", "theta"),
            P(None, None, "band", "theta"),
            P("band", "theta", None, None),
            P(),
        ),
        out_specs=(P(None, "band", "theta"), P(None, "band", "theta"), P()),
        check_vma=False,
    )
```

time: 91.1 us -> 37.1 us (0.41)
  blocking collectives: 66.6 us -> 0 us
  waiting for transfers between devices: 2.48 us -> 14.9 us
  other arithmetic: 3.72 us -> 0.09 us
  Pallas kernels: 0 us -> 3.17 us
  starting transfers between devices: 11.1 us -> 13.3 us
  between operations: 3.42 us -> 1.33 us
  local copies, waits for them, and re-layouts: 2.47 us -> 3.68 us
    psum x1 -> x0, blocking collectives: 38.4 us -> none  [on_device(): lax.psum((local_proj, jnp.sum(image * image), local_gram), ('theta', 'ban...]
    all_gather x2 -> x0, blocking collectives: 28.1 us -> none  [the longest x1 14.1 us: on_device(): lax.all_gather(low_row, 'theta', axis=1, tiled=True)]
    all_to_all x0 -> x2, waiting for transfers between devices: none -> 13.6 us  [the longest x1 7.04 us: on_device(): everyone = lax.all_to_all(copies, AXES, 0, 0, tiled=True)]
    all_to_all x0 -> x2, starting transfers between devices: none -> 8.76 us  [the longest x1 6.26 us: on_device(): everyone = lax.all_to_all(copies, AXES, 0, 0, tiled=True)]
    ppermute x6 -> x2, starting transfers between devices: 11.1 us -> 4.57 us  [the longest x1 4.08 us: on_device(): after = lax.ppermute(basis, 'theta', down)[-1].astype(jnp.bfloat16)]
    pallas_call x0 -> x2, Pallas kernels: none -> 3.17 us  [the longest x1 1.71 us: on_device(): pl.pallas_call(lambda *refs: image_kernel(theta_count, band_count, *refs)...]
    reduce_sum x5 -> x0, other arithmetic: 1.69 us -> none  [the longest x1 0.75 us: on_device(): jnp.sum(proj[:, None] * gram * proj[None, :])]
    ppermute x6 -> x2, waiting for transfers between devices: 2.48 us -> 1.3 us  [the longest x1 1.25 us: on_device(): before = lax.ppermute(basis, 'theta', up)[-1].astype(jnp.bfloat16)]
  transfers between devices with their start and end apart: 6 -> 4, of which waited for: 2 -> 3; matrix products, arithmetic and copies ran while one was open for 0% -> 2% of each run, Pallas kernels for 0% -> 0%
where the time goes in v1:
time: 37.1 us; the launch traced here: 36.8 us
  waiting for transfers between devices  14.9 us (40%)
  starting transfers between devices  13.3 us (36%)
  local copies, waits for them, and re-layouts  3.68 us (10%)
  Pallas kernels  3.17 us (9%)
  between operations  1.33 us (4%)
    all_to_all x1, waiting for transfers between devices, on_device(): everyone = lax.all_to_all(copies, AXES, 0, 0, tiled=True)  7.04 us
    all_to_all x1, waiting for transfers between devices, on_device(): sums = lax.all_to_all(partial, AXES, 0, 0, tiled=True)  6.54 us
    all_to_all x1, starting transfers between devices, on_device(): everyone = lax.all_to_all(copies, AXES, 0, 0, tiled=True)  6.26 us
    ppermute x1, starting transfers between devices, on_device(): after = lax.ppermute(basis, 'theta', down)[-1].astype(jnp.bfloat16)  4.08 us
    all_to_all x1, starting transfers between devices, on_device(): sums = lax.all_to_all(partial, AXES, 0, 0, tiled=True)  2.5 us
    unnamed x11, local copies, waits for them, and re-layouts  2.05 us
    pallas_call x1, Pallas kernels, on_device(): pl.pallas_call(lambda *refs: image_kernel(theta_count, band_count, *refs)...  1.71 us
    pallas_call x1, Pallas kernels, on_device(): pl.pallas_call(lambda *refs: finish_kernel(total, *refs), out_shape=(jax....  1.46 us
  transfers between devices with their start and end apart: 4, of which 3 were waited for; matrix products, arithmetic and copies ran while one was open for 2% of the time, Pallas kernels for 0%

profile of v1, /device:TPU:0, one launch (start us, length us, event | category | flops | bytes accessed | tf_op | source)
XLA Modules:
  0.0 36.8 jit_solution(16628938883621671819)
XLA Ops:
  0.6 0.0 copy-start
  0.6 0.0 copy-start.2
  0.7 0.8 %copy.14 = bf16[4,5,1,128]{3,1,2,0:T(8,128)(2,1)S(1)} copy(f32[4,5,1,128]{3,2,1,0:T(1,128)} %refs_2_.3) | data formatting | bytes 15360 | tf_op args[0]
  1.4 0.5 %collective-permute-start = (bf16[4,5,1,128]{3,1,2,0:T(8,128)(2,1)S(1)}, bf16[4,5,1,128]{3,1,2,0:T(8,128)(2,1)S(1)}, u32[]{:S(2)}, u32[]{:S(2)}) collective-permute-start(bf16[4,5,1,128]{3,1,2,0:T(8,128)(2,1)S(1)} %copy.14), channel_id=1, source_target_pairs={{0,4},{4,8},{8,12},{12,16},{16,20},{20,24},{24,28},{28,0},{1,5},{5... | collective-permute-start | bytes 15368 | tf_op jit(solution)/shard_map/ppermute | solution.py:103
  1.9 0.0 copy-done.2
  2.0 4.1 %collective-permute-start.1 = (bf16[4,5,1,128]{3,2,1,0:T(2,128)(2,1)S(1)}, bf16[4,5,1,128]{3,2,1,0:T(2,128)(2,1)S(1)}, u32[]{:S(2)}, u32[]{:S(2)}) collective-permute-start(bf16[4,5,1,128]{3,2,1,0:T(2,128)(2,1)S(1)} %convert.17), channel_id=1, source_target_pairs={{4,0},{8,4},{12,8},{16,12},{20,16},{24,20},{28,24},{0,28},{5,1},{9... | collective-permute-start | bytes 15368 | tf_op jit(solution)/shard_map/ppermute | solution.py:104
  6.0 1.2 %collective-permute-done = bf16[4,5,1,128]{3,1,2,0:T(8,128)(2,1)S(1)} collective-permute-done((bf16[4,5,1,128]{3,1,2,0:T(8,128)(2,1)S(1)}, bf16[4,5,1,128]{3,1,2,0:T(8,128)(2,1)S(1)}, u32[]{:S(2)}, u32[]{:S(2)}) %collective-permute-start) | collective-permute-done | bytes 5152 | tf_op jit(solution)/shard_map/ppermute | solution.py:103
  7.3 0.1 slice.19
  7.4 0.0 collective-permute-done.1
  7.4 0.1 pad_maximum_fusion
  7.5 0.0 copy-done
  7.5 0.3 fusion
  7.9 0.1 reshape.67
  7.9 0.1 broadcast_in_dim.7
  8.0 0.7 %broadcast_in_dim.8 = f32[32,5,1,128]{3,2,1,0:T(1,128)} broadcast(f32[5,128]{1,0:T(8,128)S(1)} %broadcast_in_dim.7), dimensions={1,3} | broadcast | bytes 84480 | tf_op jit(solution)/shard_map/broadcast_in_dim | solution.py:111
  8.7 6.3 %all-to-all-start = ((f32[32,5,1,128]{3,2,1,0:T(1,128)}), f32[32,5,1,128]{3,2,1,0:T(1,128)S(1)}, u32[]{:S(2)}, u32[]{:S(2)}) async-start(f32[32,5,1,128]{3,2,1,0:T(1,128)} %broadcast_in_dim.8), calls=%async_computation | async-start | bytes 163840 | tf_op jit(solution)/shard_map/all_to_all | solution.py:112
  15.6 7.0 %all-to-all-done.refs_1_ = f32[32,5,1,128]{3,2,1,0:T(1,128)S(1)} async-done(((f32[32,5,1,128]{3,2,1,0:T(1,128)}), f32[32,5,1,128]{3,2,1,0:T(1,128)S(1)}, u32[]{:S(2)}, u32[]{:S(2)}) %all-to-all-start) | async-done | bytes 81952 | tf_op jit(solution)/shard_map/all_to_all | solution.py:112
  22.7 0.0 copy-start.1
  22.7 0.6 %copy-done.1 = f32[32,5,1,128]{3,2,1,0:T(1,128)} copy-done((f32[32,5,1,128]{3,2,1,0:T(1,128)}, f32[32,5,1,128]{3,2,1,0:T(1,128)S(1)}, u32[]{:S(2)}) %copy-start.1) | copy-done | bytes 81944
  23.3 1.7 %image.1 = (f32[5,128]{1,0:T(8,128)}, f32[32,128]{1,0:T(8,128)}) custom-call(s32[1]{0:T(128)S(6)} %copy.31.refs_0_, f32[32,5,1,128]{3,2,1,0:T(1,128)} %copy-done.1, f32[4,5,1,128]{3,2,1,0:T(1,128)} %refs_2_.3, f32[5,5,1,128]{3,2,1,0:T(1,128)} %refs_3_.1, f32[4,5,1,128]{3,2,1,0:T(1,128)} %refs_4_.1), custom_call_target="tpu_custom_call" | custom-call | tf_op jit(solution)/shard_map/image/pallas_call | solution.py:116
  25.0 2.5 %all-to-all-start.1 = ((f32[32,1,128]{2,1,0:T(1,128)}), f32[32,1,128]{2,1,0:T(1,128)S(1)}, u32[]{:S(2)}, u32[]{:S(2)}) async-start(f32[32,1,128]{2,1,0:T(1,128)} %bitcast.31), calls=%async_computation.1 | async-start | bytes 32768 | tf_op jit(solution)/shard_map/all_to_all | solution.py:126
  27.5 0.7 %reshape.72 = f32[5,1,128]{2,1,0:T(1,128)} reshape(f32[5,2,64]{2,1,0:T(2,128)S(1)} %copy.15) | data formatting | bytes 5120 | tf_op jit(solution)/shard_map/reshape | solution.py:109
  28.2 6.5 %all-to-all-done.1 = f32[32,1,128]{2,1,0:T(1,128)S(1)} async-done(((f32[32,1,128]{2,1,0:T(1,128)}), f32[32,1,128]{2,1,0:T(1,128)S(1)}, u32[]{:S(2)}, u32[]{:S(2)}) %all-to-all-start.1) | async-done | bytes 16416 | tf_op jit(solution)/shard_map/all_to_all | solution.py:126
  34.7 0.0 copy-start.3
  34.7 0.6 %copy-done.3 = f32[32,1,128]{2,1,0:T(1,128)} copy-done((f32[32,1,128]{2,1,0:T(1,128)}, f32[32,1,128]{2,1,0:T(1,128)S(1)}, u32[]{:S(2)}) %copy-start.3) | copy-done | bytes 16408
  35.3 1.5 %finish.1 = (f32[5,1,128]{2,1,0:T(1,128)}, f32[1,5]{1,0:T(1,128)}) custom-call(f32[32,128]{1,0:T(8,128)} %bitcast.28, f32[5,128]{1,0:T(8,128)} %get-tuple-element.8.refs_1_, f32[4,5,1,128]{3,2,1,0:T(1,128)} %refs_2_.3), custom_call_target="tpu_custom_call" | custom-call | tf_op jit(solution)/shard_map/finish/pallas_call | solution.py:127
  (9 shorter events, 0.1 us)
Async XLA Ops:
  0.6 6.9 %copy-start = (bf16[1,2,320,640]{3,2,1,0:T(8,128)(2,1)S(1)}, bf16[1,2,320,640]{3,2,1,0:T(8,128)(2,1)}, u32[]{:S(2)}) copy-start(bf16[1,2,320,640]{3,2,1,0:T(8,128)(2,1)} %param.8) | copy-start | bytes 2457604
  0.6 1.3 %copy-start.2 = (f32[4,5,1,128]{3,2,1,0:T(1,128)S(1)}, f32[4,5,1,128]{3,2,1,0:T(1,128)}, u32[]{:S(2)}) copy-start(f32[4,5,1,128]{3,2,1,0:T(1,128)} %refs_2_.3) | copy-start | bytes 30724
  1.4 5.8 %collective-permute-start = (bf16[4,5,1,128]{3,1,2,0:T(8,128)(2,1)S(1)}, bf16[4,5,1,128]{3,1,2,0:T(8,128)(2,1)S(1)}, u32[]{:S(2)}, u32[]{:S(2)}) collective-permute-start(bf16[4,5,1,128]{3,1,2,0:T(8,128)(2,1)S(1)} %copy.14), channel_id=1, source_target_pairs={{0,4},{4,8},{8,12},{12,16},{16,20},{20,24},{24,28},{28,0},{1,5},{5... | collective-permute-start | bytes 15368 | tf_op jit(solution)/shard_map/ppermute | solution.py:103
  2.0 5.5 %collective-permute-start.1 = (bf16[4,5,1,128]{3,2,1,0:T(2,128)(2,1)S(1)}, bf16[4,5,1,128]{3,2,1,0:T(2,128)(2,1)S(1)}, u32[]{:S(2)}, u32[]{:S(2)}) collective-permute-start(bf16[4,5,1,128]{3,2,1,0:T(2,128)(2,1)S(1)} %convert.17), channel_id=1, source_target_pairs={{4,0},{8,4},{12,8},{16,12},{20,16},{24,20},{28,24},{0,28},{5,1},{9... | collective-permute-start | bytes 15368 | tf_op jit(solution)/shard_map/ppermute | solution.py:104
  8.7 14.0 %all-to-all-start = ((f32[32,5,1,128]{3,2,1,0:T(1,128)}), f32[32,5,1,128]{3,2,1,0:T(1,128)S(1)}, u32[]{:S(2)}, u32[]{:S(2)}) async-start(f32[32,5,1,128]{3,2,1,0:T(1,128)} %broadcast_in_dim.8), calls=%async_computation | async-start | bytes 163840 | tf_op jit(solution)/shard_map/all_to_all | solution.py:112
  22.7 0.6 %copy-start.1 = (f32[32,5,1,128]{3,2,1,0:T(1,128)}, f32[32,5,1,128]{3,2,1,0:T(1,128)S(1)}, u32[]{:S(2)}) copy-start(f32[32,5,1,128]{3,2,1,0:T(1,128)S(1)} %all-to-all-done.refs_1_) | copy-start | bytes 245764
  25.0 9.7 %all-to-all-start.1 = ((f32[32,1,128]{2,1,0:T(1,128)}), f32[32,1,128]{2,1,0:T(1,128)S(1)}, u32[]{:S(2)}, u32[]{:S(2)}) async-start(f32[32,1,128]{2,1,0:T(1,128)} %bitcast.31), calls=%async_computation.1 | async-start | bytes 32768 | tf_op jit(solution)/shard_map/all_to_all | solution.py:126
  34.7 0.6 %copy-start.3 = (f32[32,1,128]{2,1,0:T(1,128)}, f32[32,1,128]{2,1,0:T(1,128)S(1)}, u32[]{:S(2)}) copy-start(f32[32,1,128]{2,1,0:T(1,128)S(1)} %all-to-all-done.1) | copy-start | bytes 49156

commit v2 on v1

--- a/solution.py
+++ b/solution.py
@@ -116,13 +116,13 @@
     image, partial = pl.pallas_call(
         lambda *refs: image_kernel(theta_count, band_count, *refs),
         out_shape=(
-            jax.ShapeDtypeStruct((ncomp, width), jnp.float32),
-            jax.ShapeDtypeStruct((devices, width), jnp.float32),
+            pltpu.VMEM((ncomp, width), jnp.float32),
+            pltpu.VMEM((devices, width), jnp.float32),
         ),
         in_specs=[smem, vmem, vmem, vmem, vmem],
         out_specs=(vmem, vmem),
         name="image",
-    )(rotor_offset, everyone, basis, jac_block, face_coef)
+    )(rotor_offset, *[pltpu.with_memory_space_constraint(v, pltpu.VMEM) for v in (everyone, basis, jac_block, face_coef)])
     sums = lax.all_to_all(partial, AXES, 0, 0, tiled=True)
     v_next, hess = pl.pallas_call(
         lambda *refs: finish_kernel(total, *refs),
@@ -133,7 +133,7 @@
         in_specs=[vmem, vmem, vmem],
         out_specs=(vmem, vmem),
         name="finish",
-    )(sums, image, basis)
+    )(*[pltpu.with_memory_space_constraint(v, pltpu.VMEM) for v in (sums, image, basis)])
     return precond, v_next, hess.reshape(kb + 1)
 
 

time: 37.1 us -> 34.3 us (0.925)
  Pallas kernels: 3.17 us -> 1.54 us
  local copies, waits for them, and re-layouts: 3.68 us -> 2.46 us
    unnamed x11, local copies, waits for them, and re-layouts: 2.05 us -> 0.82 us
    pallas_call x1, Pallas kernels: 1.71 us -> 0.81 us  [on_device(): pl.pallas_call(lambda *refs: image_kernel(theta_count, band_count, *refs)...]
    pallas_call x1, Pallas kernels: 1.46 us -> 0.74 us  [on_device(): pl.pallas_call(lambda *refs: finish_kernel(total, *refs), out_shape=(jax....]
where the time goes in v2:
time: 34.3 us; the launch traced here: 34 us
  waiting for transfers between devices  14.9 us (43%)
  starting transfers between devices  13.4 us (39%)
  local copies, waits for them, and re-layouts  2.46 us (7%)
  Pallas kernels  1.54 us (4%)
  between operations  1.33 us (4%)
    all_to_all x1, waiting for transfers between devices, on_device(): everyone = lax.all_to_all(copies, AXES, 0, 0, tiled=True)  7.04 us
    all_to_all x1, waiting for transfers between devices, on_device(): sums = lax.all_to_all(partial, AXES, 0, 0, tiled=True)  6.53 us
    all_to_all x1, starting transfers between devices, on_device(): everyone = lax.all_to_all(copies, AXES, 0, 0, tiled=True)  6.26 us
    ppermute x1, starting transfers between devices, on_device(): after = lax.ppermute(basis, 'theta', down)[-1].astype(jnp.bfloat16)  4.08 us
    all_to_all x1, starting transfers between devices, on_device(): sums = lax.all_to_all(partial, AXES, 0, 0, tiled=True)  2.55 us
    ppermute x1, waiting for transfers between devices, on_device(): before = lax.ppermute(basis, 'theta', up)[-1].astype(jnp.bfloat16)  1.25 us
    unnamed x11, local copies, waits for them, and re-layouts  0.82 us
    pallas_call x1, Pallas kernels, on_device(): pl.pallas_call(lambda *refs: image_kernel(theta_count, band_count, *refs)...  0.81 us
  transfers between devices with their start and end apart: 4, of which 3 were waited for; matrix products, arithmetic and copies ran while one was open for 2% of the time, Pallas kernels for 0%

profile of v2, /device:TPU:0, one launch (start us, length us, event | category | flops | bytes accessed | tf_op | source)
XLA Modules:
  0.0 34.0 jit_solution(3251136753719986115)
XLA Ops:
  0.6 0.0 copy-start
  0.6 0.0 copy-start.1
  0.7 0.8 %copy.14 = bf16[4,5,1,128]{3,1,2,0:T(8,128)(2,1)S(1)} copy(f32[4,5,1,128]{3,2,1,0:T(1,128)} %refs_2_.3) | data formatting | bytes 15360 | tf_op args[0]
  1.4 0.5 %collective-permute-start = (bf16[4,5,1,128]{3,1,2,0:T(8,128)(2,1)S(1)}, bf16[4,5,1,128]{3,1,2,0:T(8,128)(2,1)S(1)}, u32[]{:S(2)}, u32[]{:S(2)}) collective-permute-start(bf16[4,5,1,128]{3,1,2,0:T(8,128)(2,1)S(1)} %copy.14), channel_id=1, source_target_pairs={{0,4},{4,8},{8,12},{12,16},{16,20},{20,24},{24,28},{28,0},{1,5},{5... | collective-permute-start | bytes 15368 | tf_op jit(solution)/shard_map/ppermute | solution.py:103
  1.9 0.0 copy-done.1
  1.9 4.1 %collective-permute-start.1 = (bf16[4,5,1,128]{3,2,1,0:T(2,128)(2,1)S(1)}, bf16[4,5,1,128]{3,2,1,0:T(2,128)(2,1)S(1)}, u32[]{:S(2)}, u32[]{:S(2)}) collective-permute-start(bf16[4,5,1,128]{3,2,1,0:T(2,128)(2,1)S(1)} %convert.17), channel_id=1, source_target_pairs={{4,0},{8,4},{12,8},{16,12},{20,16},{24,20},{28,24},{0,28},{5,1},{9... | collective-permute-start | bytes 15368 | tf_op jit(solution)/shard_map/ppermute | solution.py:104
  6.0 1.2 %collective-permute-done = bf16[4,5,1,128]{3,1,2,0:T(8,128)(2,1)S(1)} collective-permute-done((bf16[4,5,1,128]{3,1,2,0:T(8,128)(2,1)S(1)}, bf16[4,5,1,128]{3,1,2,0:T(8,128)(2,1)S(1)}, u32[]{:S(2)}, u32[]{:S(2)}) %collective-permute-start) | collective-permute-done | bytes 5152 | tf_op jit(solution)/shard_map/ppermute | solution.py:103
  7.3 0.1 slice.19
  7.4 0.0 collective-permute-done.1
  7.4 0.1 pad_maximum_fusion
  7.5 0.0 copy-done
  7.5 0.3 fusion
  7.9 0.1 reshape.67
  7.9 0.1 broadcast_in_dim.7
  8.0 0.7 %broadcast_in_dim.8 = f32[32,5,1,128]{3,2,1,0:T(1,128)} broadcast(f32[5,128]{1,0:T(8,128)S(1)} %broadcast_in_dim.7), dimensions={1,3} | broadcast | bytes 84480 | tf_op jit(solution)/shard_map/broadcast_in_dim | solution.py:111
  8.7 0.0 copy-start.2
  8.7 0.0 copy-start.3
  8.7 6.3 %all-to-all-start = ((f32[32,5,1,128]{3,2,1,0:T(1,128)}), f32[32,5,1,128]{3,2,1,0:T(1,128)S(1)}, u32[]{:S(2)}, u32[]{:S(2)}) async-start(f32[32,5,1,128]{3,2,1,0:T(1,128)} %broadcast_in_dim.8), calls=%async_computation | async-start | bytes 163840 | tf_op jit(solution)/shard_map/all_to_all | solution.py:112
  15.6 7.0 %all-to-all-done.refs_1_ = f32[32,5,1,128]{3,2,1,0:T(1,128)S(1)} async-done(((f32[32,5,1,128]{3,2,1,0:T(1,128)}), f32[32,5,1,128]{3,2,1,0:T(1,128)S(1)}, u32[]{:S(2)}, u32[]{:S(2)}) %all-to-all-start) | async-done | bytes 81952 | tf_op jit(solution)/shard_map/all_to_all | solution.py:112
  22.7 0.0 copy-done.2
  22.7 0.0 copy-done.3
  22.7 0.8 %image.1 = (f32[5,128]{1,0:T(8,128)S(1)}, f32[32,128]{1,0:T(8,128)}) custom-call(s32[1]{0:T(128)S(6)} %copy.31.refs_0_, f32[32,5,1,128]{3,2,1,0:T(1,128)S(1)} %all-to-all-done.refs_1_, f32[4,5,1,128]{3,2,1,0:T(1,128)S(1)} %copy-done.1, f32[5,5,1,128]{3,2,1,0:T(1,128)S(1)} %copy-done.2, f32[4,5,1,128]{3,2,1,0:T(1,128)S(1)} %copy-done.3), custom_call_target="tpu_custom_call" | custom-call | tf_op jit(solution)/shard_map/image/pallas_call | solution.py:116
  23.5 2.6 %all-to-all-start.1 = ((f32[32,1,128]{2,1,0:T(1,128)}), f32[32,1,128]{2,1,0:T(1,128)S(1)}, u32[]{:S(2)}, u32[]{:S(2)}) async-start(f32[32,1,128]{2,1,0:T(1,128)} %bitcast.8), calls=%async_computation.1 | async-start | bytes 32768 | tf_op jit(solution)/shard_map/all_to_all | solution.py:126
  26.1 0.7 %reshape.72 = f32[5,1,128]{2,1,0:T(1,128)} reshape(f32[5,2,64]{2,1,0:T(2,128)S(1)} %copy.15) | data formatting | bytes 5120 | tf_op jit(solution)/shard_map/reshape | solution.py:109
  26.7 6.5 %all-to-all-done.1 = f32[32,1,128]{2,1,0:T(1,128)S(1)} async-done(((f32[32,1,128]{2,1,0:T(1,128)}), f32[32,1,128]{2,1,0:T(1,128)S(1)}, u32[]{:S(2)}, u32[]{:S(2)}) %all-to-all-start.1) | async-done | bytes 16416 | tf_op jit(solution)/shard_map/all_to_all | solution.py:126
  33.2 0.7 %finish.1 = (f32[5,1,128]{2,1,0:T(1,128)}, f32[1,5]{1,0:T(1,128)}) custom-call(f32[32,128]{1,0:T(8,128)S(1)} %bitcast.28, f32[5,128]{1,0:T(8,128)S(1)} %get-tuple-element.8.refs_1_, f32[4,5,1,128]{3,2,1,0:T(1,128)S(1)} %copy-done.1), custom_call_target="tpu_custom_call" | custom-call | tf_op jit(solution)/shard_map/finish/pallas_call | solution.py:127
  (9 shorter events, 0.1 us)
Async XLA Ops:
  0.6 6.9 %copy-start = (bf16[1,2,320,640]{3,2,1,0:T(8,128)(2,1)S(1)}, bf16[1,2,320,640]{3,2,1,0:T(8,128)(2,1)}, u32[]{:S(2)}) copy-start(bf16[1,2,320,640]{3,2,1,0:T(8,128)(2,1)} %param.8) | copy-start | bytes 2457604
  0.6 1.3 %copy-start.1 = (f32[4,5,1,128]{3,2,1,0:T(1,128)S(1)}, f32[4,5,1,128]{3,2,1,0:T(1,128)}, u32[]{:S(2)}) copy-start(f32[4,5,1,128]{3,2,1,0:T(1,128)} %refs_2_.3) | copy-start | bytes 30724
  1.4 5.8 %collective-permute-start = (bf16[4,5,1,128]{3,1,2,0:T(8,128)(2,1)S(1)}, bf16[4,5,1,128]{3,1,2,0:T(8,128)(2,1)S(1)}, u32[]{:S(2)}, u32[]{:S(2)}) collective-permute-start(bf16[4,5,1,128]{3,1,2,0:T(8,128)(2,1)S(1)} %copy.14), channel_id=1, source_target_pairs={{0,4},{4,8},{8,12},{12,16},{16,20},{20,24},{24,28},{28,0},{1,5},{5... | collective-permute-start | bytes 15368 | tf_op jit(solution)/shard_map/ppermute | solution.py:103
  1.9 5.5 %collective-permute-start.1 = (bf16[4,5,1,128]{3,2,1,0:T(2,128)(2,1)S(1)}, bf16[4,5,1,128]{3,2,1,0:T(2,128)(2,1)S(1)}, u32[]{:S(2)}, u32[]{:S(2)}) collective-permute-start(bf16[4,5,1,128]{3,2,1,0:T(2,128)(2,1)S(1)} %convert.17), channel_id=1, source_target_pairs={{4,0},{8,4},{12,8},{16,12},{20,16},{24,20},{28,24},{0,28},{5,1},{9... | collective-permute-start | bytes 15368 | tf_op jit(solution)/shard_map/ppermute | solution.py:104
  8.7 14.0 %copy-start.2 = (f32[5,5,1,128]{3,2,1,0:T(1,128)S(1)}, f32[5,5,1,128]{3,2,1,0:T(1,128)}, u32[]{:S(2)}) copy-start(f32[5,5,1,128]{3,2,1,0:T(1,128)} %refs_3_.1) | copy-start | bytes 38404
  8.7 14.0 %copy-start.3 = (f32[4,5,1,128]{3,2,1,0:T(1,128)S(1)}, f32[4,5,1,128]{3,2,1,0:T(1,128)}, u32[]{:S(2)}) copy-start(f32[4,5,1,128]{3,2,1,0:T(1,128)} %refs_4_.1) | copy-start | bytes 30724
  8.7 14.0 %all-to-all-start = ((f32[32,5,1,128]{3,2,1,0:T(1,128)}), f32[32,5,1,128]{3,2,1,0:T(1,128)S(1)}, u32[]{:S(2)}, u32[]{:S(2)}) async-start(f32[32,5,1,128]{3,2,1,0:T(1,128)} %broadcast_in_dim.8), calls=%async_computation | async-start | bytes 163840 | tf_op jit(solution)/shard_map/all_to_all | solution.py:112
  23.5 9.8 %all-to-all-start.1 = ((f32[32,1,128]{2,1,0:T(1,128)}), f32[32,1,128]{2,1,0:T(1,128)S(1)}, u32[]{:S(2)}, u32[]{:S(2)}) async-start(f32[32,1,128]{2,1,0:T(1,128)} %bitcast.8), calls=%async_computation.1 | async-start | bytes 32768 | tf_op jit(solution)/shard_map/all_to_all | solution.py:126

commit v3 on v2

v3 whole, which is shorter than its diff:
```python
import jax
import jax.numpy as jnp
from jax import lax
from jax.experimental import pallas as pl
from jax.experimental.pallas import tpu as pltpu
from jax.sharding import PartitionSpec as P

AXES = ("theta", "band")
MERGED_LIMIT = 64
THIRD = 32


def even(count):
    return -(-count // 2) * 2


def in_vmem(*arrays):
    return [pltpu.with_memory_space_constraint(array, pltpu.VMEM) for array in arrays]


def specs(count, scalars=0):
    smem = pl.BlockSpec(memory_space=pltpu.SMEM)
    vmem = pl.BlockSpec(memory_space=pltpu.VMEM)
    return [smem] * scalars + [vmem] * count


def lane_reduced(rows):
    count, width = rows.shape
    sums = jnp.sum(rows, axis=1, keepdims=True)
    row = lax.broadcasted_iota(jnp.int32, (count, width), 0)
    lane = lax.broadcasted_iota(jnp.int32, (count, width), 1)
    return jnp.sum(jnp.where(row == lane, sums, 0.0), axis=0, keepdims=True)


def coupled(jac_ref, precond):
    out = jac_ref[:, 0, 0, :] * precond[0:1]
    for w in range(1, precond.shape[0]):
        out += jac_ref[:, w, 0, :] * precond[w : w + 1]
    return out


def over_cells(arrays):
    return [jnp.sum(array, axis=0, keepdims=True) for array in arrays]


def finished(proj, gram, square, image, basis_ref, next_ref, hess_ref):
    kb = basis_ref.shape[0]
    squares = square
    for i in range(kb):
        squares -= 2.0 * proj[i] * proj[i]
    for i in range(kb):
        for j in range(kb):
            squares += proj[i] * gram[i * kb + j] * proj[j]
    drop = proj[0] * basis_ref[0, :, 0, :]
    for i in range(1, kb):
        drop += proj[i] * basis_ref[i, :, 0, :]
    row = (1, image.shape[1])
    hnorm = jnp.sqrt(jnp.full(row, squares + 1e-06, jnp.float32))
    next_ref[:, 0, :] = (image - drop) / hnorm
    lane = lax.broadcasted_iota(jnp.int32, row, 1)
    hess = hnorm
    for i in range(kb):
        hess = jnp.where(lane == i, proj[i], hess)
    hess_ref[...] = hess[:, : kb + 1]


def image_kernel(theta_count, band_count, offset_ref, all_ref, basis_ref, jac_ref, face_ref, image_ref, send_ref):
    kb, ncomp, _, width = basis_ref.shape
    cycle = theta_count * width
    middle = band_count // 2
    theta = lax.axis_index("theta")
    band = lax.axis_index("band")
    offset = offset_ref[0]

    def cells_of(t, b):
        t = jnp.where(t >= theta_count, t - theta_count, t)
        return all_ref[t * band_count + b].reshape(ncomp, width)

    lane = lax.broadcasted_iota(jnp.int32, (ncomp, width), 1)

    def shifted(row, shift):
        start = theta * width + shift
        first = lax.rem(start // width, theta_count)
        skip = lax.rem(start, width)
        back = lax.rem(width - skip, width)
        one = pltpu.roll(cells_of(first, row), back, 1)
        two = pltpu.roll(cells_of(first + 1, row), back, 1)
        return jnp.where(lane < width - skip, one, two)

    precond = cells_of(theta, band)
    before = cells_of(theta + theta_count - 1, band)
    after = cells_of(theta + 1, band)
    theta_minus = jnp.where(lane == 0, pltpu.roll(before, 1, 1), pltpu.roll(precond, 1, 1))
    theta_plus = jnp.where(lane == width - 1, pltpu.roll(after, width - 1, 1), pltpu.roll(precond, width - 1, 1))
    up_shift = jnp.where(band == middle - 1, offset, 0)
    low_shift = jnp.where(band == middle, cycle - offset, 0)
    band_plus = shifted(jnp.minimum(band + 1, band_count - 1), up_shift)
    band_plus = jnp.where(band == band_count - 1, 0.0, band_plus)
    band_minus = shifted(jnp.maximum(band - 1, 0), low_shift)
    band_minus = jnp.where(band == 0, 0.0, band_minus)
    image = 6.0 * precond + coupled(jac_ref, precond)
    image = image - (
        face_ref[0, :, 0, :] * theta_minus
        + face_ref[1, :, 0, :] * theta_plus
        + face_ref[2, :, 0, :] * band_minus
        + face_ref[3, :, 0, :] * band_plus
    )
    image_ref[...] = image
    vectors = [basis_ref[i, :, 0, :] for i in range(kb)]
    pairs = [vectors[i] * image for i in range(kb)] + [image * image]
    pairs += [vectors[i] * vectors[j] for i in range(kb) for j in range(kb)]
    rows = jnp.concatenate(over_cells(pairs), axis=0)
    send_ref[...] = jnp.broadcast_to(lane_reduced(rows), send_ref.shape)


def finish_kernel(total, sums_ref, image_ref, basis_ref, next_ref, hess_ref):
    kb = basis_ref.shape[0]
    sums = jnp.sum(sums_ref[...], axis=0, keepdims=True) / total
    proj = [sums[0, i] for i in range(kb)]
    gram = [sums[0, kb + 1 + i] for i in range(kb * kb)]
    finished(proj, gram, sums[0, kb], image_ref[...], basis_ref, next_ref, hess_ref)


def two_exchanges(precond, basis, jac_block, face_coef, rotor_offset):
    kb, ncomp, _, width = basis.shape
    theta_count = lax.axis_size("theta")
    band_count = lax.axis_size("band")
    devices = theta_count * band_count
    copies = jnp.broadcast_to(precond[None], (devices, ncomp, 1, width))
    everyone = lax.all_to_all(copies, AXES, 0, 0, tiled=True)
    image, partial = pl.pallas_call(
        lambda *refs: image_kernel(theta_count, band_count, *refs),
        out_shape=(pltpu.VMEM((ncomp, width), jnp.float32), pltpu.VMEM((devices, width), jnp.float32)),
        in_specs=specs(4, 1),
        out_specs=specs(2),
        name="image",
    )(rotor_offset, *in_vmem(everyone, basis, jac_block, face_coef))
    sums = lax.all_to_all(partial, AXES, 0, 0, tiled=True)
    total = ncomp * devices * width
    return pl.pallas_call(
        lambda *refs: finish_kernel(total, *refs),
        out_shape=(
            jax.ShapeDtypeStruct((ncomp, 1, width), jnp.float32),
            jax.ShapeDtypeStruct((1, kb + 1), jnp.float32),
        ),
        in_specs=specs(3),
        out_specs=specs(2),
        name="finish",
    )(*in_vmem(sums, image, basis))


def thirds(x):
    high = x.astype(jnp.bfloat16).astype(jnp.float32)
    middle = (x - high).astype(jnp.bfloat16).astype(jnp.float32)
    return high, middle, x - high - middle


def message_rows(kb, ncomp):
    return even((4 + kb) * ncomp + 1)


def local_kernel(precond_ref, basis_ref, jac_ref, face_ref, send_ref, inner_ref, out_ref):
    kb, ncomp, _, width = basis_ref.shape
    slot = message_rows(kb, ncomp)
    precond = precond_ref[...]
    out_ref[:, 0, :] = precond
    lane = lax.broadcasted_iota(jnp.int32, (ncomp, width), 1)
    lower = jnp.where(lane == 0, 0.0, pltpu.roll(precond, 1, 1))
    upper = jnp.where(lane == width - 1, 0.0, pltpu.roll(precond, width - 1, 1))
    inner = 6.0 * precond + coupled(jac_ref, precond)
    inner = inner - (face_ref[0, :, 0, :] * lower + face_ref[1, :, 0, :] * upper)
    inner_ref[...] = inner
    vectors = [basis_ref[i, :, 0, :] for i in range(kb)]
    pairs = [vectors[i] * inner for i in range(kb)] + [inner * inner]
    pairs += [vectors[i] * vectors[j] for i in range(kb) for j in range(kb)]
    rows = jnp.concatenate(over_cells(pairs), axis=0)
    high, middle, low = thirds(lane_reduced(rows))
    sums = high + pltpu.roll(middle, THIRD, 1) + pltpu.roll(low, 2 * THIRD, 1)
    row = lax.broadcasted_iota(jnp.int32, (ncomp, width), 0)
    first = jnp.where(lane == 3 * THIRD + row, face_ref[0, :, 0, :][:, :1], 0.0)
    last = jnp.where(lane == 3 * THIRD + THIRD // 2 + row, face_ref[1, :, 0, :][:, width - 1 :], 0.0)
    sums += jnp.sum(first + last, axis=0, keepdims=True)
    groups = [face_ref[2, :, 0, :], face_ref[3, :, 0, :], *vectors, inner, precond, sums]
    if slot > (4 + kb) * ncomp + 1:
        groups.append(jnp.zeros((slot - (4 + kb) * ncomp - 1, width), jnp.float32))
    message = jnp.concatenate(groups, axis=0).astype(jnp.bfloat16)
    for device in range(send_ref.shape[0] // slot):
        send_ref[device * slot : (device + 1) * slot] = message


def merged_kernel(theta_count, band_count, offset_ref, all_ref, inner_ref, basis_ref, face_ref, next_ref, hess_ref, own_ref):
    kb, ncomp, _, width = basis_ref.shape
    devices = theta_count * band_count
    cycle = theta_count * width
    total = ncomp * devices * width
    middle = band_count // 2
    shape = (devices, width)
    row = lax.broadcasted_iota(jnp.int32, shape, 0)
    lane = lax.broadcasted_iota(jnp.int32, shape, 1)
    band = lax.rem(row, band_count)
    here = lax.axis_index("theta") * band_count + lax.axis_index("band")
    base = cycle // 2 - width
    start = offset_ref[0] - base
    late = start >= width
    skip = jnp.where(late, start - width, start)

    def part(place):
        return all_ref[pl.ds(place, devices, stride=all_ref.shape[0] // devices), :]

    def rows_up(x, count):
        return pltpu.roll(x, (devices - count) % devices, 0)

    half = theta_count // 2
    local = part((4 + kb) * ncomp)
    square = jnp.zeros(shape, jnp.float32)
    cross = [jnp.zeros(shape, jnp.float32) for _ in range(kb)]
    for u in range(ncomp):
        inner, precond = part((2 + kb) * ncomp + u), part((3 + kb) * ncomp + u)
        turned = pltpu.roll(precond, lax.rem(width - skip, width), 1)
        near, at, far = (rows_up(turned, (half + k) * band_count + 1) for k in (-1, 0, 1))
        split = lane < width - skip
        rotor_up = jnp.where(split, jnp.where(late, at, near), jnp.where(late, far, at))
        turned = pltpu.roll(precond, skip, 1)
        near, at, far = (rows_up(turned, (-half + k) * band_count - 1) for k in (1, 0, -1))
        split = lane >= skip
        rotor_down = jnp.where(split, jnp.where(late, at, near), jnp.where(late, far, at))
        band_plus = jnp.where(band == middle - 1, rotor_up, rows_up(precond, 1))
        band_plus = jnp.where(band == band_count - 1, 0.0, band_plus)
        band_minus = jnp.where(band == middle, rotor_down, rows_up(precond, -1))
        band_minus = jnp.where(band == 0, 0.0, band_minus)
        before = rows_up(pltpu.roll(precond, 1, 1), -band_count)
        after = rows_up(pltpu.roll(precond, width - 1, 1), band_count)
        edge = jnp.where(lane == 0, before, after)
        place = 3 * THIRD + u
        first = pltpu.roll(local, width - place, 1)
        last = pltpu.roll(local, width - 1 - place - THIRD // 2, 1)
        coef = jnp.where(lane == 0, first, jnp.where(lane == width - 1, last, 0.0))
        own_ref[0, u] = band_minus
        own_ref[1, u] = band_plus
        own_ref[2, u] = edge
        outer = part(u) * band_minus + part(ncomp + u) * band_plus + coef * edge
        square += outer * (outer - 2.0 * inner)
        for i in range(kb):
            cross[i] += part((2 + i) * ncomp + u) * outer
    local = jnp.sum(local, axis=0, keepdims=True) / total
    local = local + pltpu.roll(local, width - THIRD, 1) + pltpu.roll(local, width - 2 * THIRD, 1)
    sums = lane_reduced(jnp.concatenate(over_cells(cross + [square]), axis=0)) / total
    proj = [local[0, i] - sums[0, i] for i in range(kb)]
    gram = [local[0, kb + 1 + i] for i in range(kb * kb)]

    def own(k):
        return own_ref[k, :, pl.ds(here, 1), :].reshape(ncomp, width)

    lane = lax.broadcasted_iota(jnp.int32, (ncomp, width), 1)
    edges = jnp.where(lane == 0, face_ref[0, :, 0, :], jnp.where(lane == width - 1, face_ref[1, :, 0, :], 0.0))
    outer = face_ref[2, :, 0, :] * own(0) + face_ref[3, :, 0, :] * own(1) + edges * own(2)
    finished(proj, gram, local[0, kb] + sums[0, kb], inner_ref[...] - outer, basis_ref, next_ref, hess_ref)


def one_exchange(precond, basis, jac_block, face_coef, rotor_offset):
    kb, ncomp, _, width = basis.shape
    theta_count = lax.axis_size("theta")
    band_count = lax.axis_size("band")
    devices = theta_count * band_count
    send, inner, precond = pl.pallas_call(
        local_kernel,
        out_shape=(
            jax.ShapeDtypeStruct((devices * message_rows(kb, ncomp), width), jnp.bfloat16),
            pltpu.VMEM((ncomp, width), jnp.float32),
            jax.ShapeDtypeStruct((ncomp, 1, width), jnp.float32),
        ),
        in_specs=specs(4),
        out_specs=specs(3),
        name="local",
    )(*in_vmem(precond.reshape(ncomp, width), basis, jac_block, face_coef))
    everyone = exchanged(send, devices)
    everyone = everyone.astype(jnp.float32)
    v_next, hess = pl.pallas_call(
        lambda *refs: merged_kernel(theta_count, band_count, *refs),
        out_shape=(
            jax.ShapeDtypeStruct((ncomp, 1, width), jnp.float32),
            jax.ShapeDtypeStruct((1, kb + 1), jnp.float32),
        ),
        in_specs=specs(4, 1),
        out_specs=specs(2),
        scratch_shapes=[pltpu.VMEM((3, ncomp, devices, width), jnp.float32)],
        name="merged",
    )(rotor_offset, *in_vmem(everyone, inner, basis, face_coef))
    return precond, v_next, hess


def exchanged(rows, devices):
    slots = rows.reshape(devices, -1, 2, rows.shape[-1])
    return lax.all_to_all(slots, AXES, 0, 0, tiled=True).reshape(rows.shape)


def on_device(basis, jac_block, face_coef, panel_inverse, rotor_offset):
    kb, ncomp, rows_here, width = basis.shape
    assert rows_here == 1
    half = width // 2
    theta_count = lax.axis_size("theta")
    band_count = lax.axis_size("band")
    merged = theta_count * band_count <= MERGED_LIMIT
    up = [(i, (i + 1) % theta_count) for i in range(theta_count)]
    down = [(j, i) for i, j in up]
    before = lax.ppermute(basis, "theta", up)
    after = lax.ppermute(basis, "theta", down)
    before, current, after = (x[-1].astype(jnp.bfloat16) for x in (before, basis, after))
    extended = jnp.concatenate([before[..., half:], current, after[..., :half]], axis=2)
    panels = extended.reshape(ncomp, 2, width).transpose(1, 0, 2).reshape(2, ncomp * width)
    owned = jnp.einsum("pij,pj->pi", panel_inverse[0], panels, preferred_element_type=jnp.float32)
    precond = owned.reshape(2, ncomp, half).transpose(1, 0, 2).reshape(ncomp, 1, width)
    if merged:
        precond, v_next, hess = one_exchange(precond, basis, jac_block, face_coef, rotor_offset)
    else:
        v_next, hess = two_exchanges(precond, basis, jac_block, face_coef, rotor_offset)
    return precond, v_next, hess.reshape(kb + 1)


def solution(mesh):
    return jax.shard_map(
        on_device,
        mesh=mesh,
        in_specs=(
            P(None, None, "band", "theta"),
            P(None, None, "band", "theta"),
            P(None, None, "band", "theta"),
            P("band", "theta", None, None),
            P(),
        ),
        out_specs=(P(None, "band", "theta"), P(None, "band", "theta"), P()),
        check_vma=False,
    )
```

time: 34.3 us -> 30.1 us (0.88)
  starting transfers between devices: 13.4 us -> 7.33 us
  waiting for transfers between devices: 14.9 us -> 16.8 us
  local copies, waits for them, and re-layouts: 2.46 us -> 0.95 us
  other arithmetic: 0.09 us -> 0.91 us
  Pallas kernels: 1.54 us -> 2.05 us
    all_to_all x2 -> x1, starting transfers between devices: 8.81 us -> 2.81 us  [exchanged(): return lax.all_to_all(slots, AXES, 0, 0, tiled=True).reshape(rows.shape)]
    ppermute x2, waiting for transfers between devices: 1.3 us -> 4.83 us  [the longest x1 3.48 us: on_device(): before = lax.ppermute(basis, 'theta', up)]
    all_to_all x2 -> x1, waiting for transfers between devices: 13.6 us -> 11.9 us  [exchanged(): return lax.all_to_all(slots, AXES, 0, 0, tiled=True).reshape(rows.shape)]
    unnamed x1, other arithmetic: 0.01 us -> 0.79 us
    broadcast_in_dim x2 -> x0, local copies, waits for them, and re-layouts: 0.78 us -> none  [on_device(): copies = jnp.broadcast_to(precond[None], (devices, ncomp, 1, width))]
    reshape x2 -> x1, local copies, waits for them, and re-layouts: 0.74 us -> 0.08 us  [on_device(): owned.reshape(2, ncomp, half).transpose(1, 0, 2).reshape(ncomp, 1, width)]
    pallas_call x2, Pallas kernels: 1.54 us -> 2.05 us  [the longest x1 1.05 us: one_exchange(): pl.pallas_call(lambda *refs: merged_kernel(theta_count, band_count, *refs...]
  transfers between devices with their start and end apart: 4 -> 3, of which waited for: 3 -> 3; matrix products, arithmetic and copies ran while one was open for 2% -> 0% of each run, Pallas kernels for 0% -> 0%
where the time goes in v3:
time: 30.1 us; the launch traced here: 29.7 us
  waiting for transfers between devices  16.8 us (56%)
  starting transfers between devices  7.33 us (24%)
  Pallas kernels  2.05 us (7%)
  between operations  1.34 us (4%)
  local copies, waits for them, and re-layouts  0.95 us (3%)
  other arithmetic  0.91 us (3%)
  matrix products  0.32 us (1%)
    all_to_all x1, waiting for transfers between devices, exchanged(): return lax.all_to_all(slots, AXES, 0, 0, tiled=True).reshape(rows.shape)  11.9 us
    ppermute x1, starting transfers between devices, on_device(): after = lax.ppermute(basis, 'theta', down)  4.52 us
    ppermute x1, waiting for transfers between devices, on_device(): before = lax.ppermute(basis, 'theta', up)  3.48 us
    all_to_all x1, starting transfers between devices, exchanged(): return lax.all_to_all(slots, AXES, 0, 0, tiled=True).reshape(rows.shape)  2.81 us
    ppermute x1, waiting for transfers between devices, on_device(): after = lax.ppermute(basis, 'theta', down)  1.35 us
    pallas_call x1, Pallas kernels, one_exchange(): pl.pallas_call(lambda *refs: merged_kernel(theta_count, band_count, *refs...  1.05 us
    pallas_call x1, Pallas kernels, one_exchange(): pl.pallas_call(local_kernel, out_shape=(jax.ShapeDtypeStruct((devices * m...  1 us
    unnamed x1, other arithmetic  0.79 us
  transfers between devices with their start and end apart: 3, of which 3 were waited for; matrix products, arithmetic and copies ran while one was open for 0% of the time, Pallas kernels for 0%

profile of v3, /device:TPU:0, one launch (start us, length us, event | category | flops | bytes accessed | tf_op | source)
XLA Modules:
  0.0 29.7 jit_solution(6970459748896579703)
XLA Ops:
  0.6 0.0 copy-start
  0.6 0.0 copy-start.1
  0.7 0.8 %convert.19 = bf16[4,5,1,128]{3,2,1,0:T(2,128)(2,1)S(1)} convert(f32[4,5,1,128]{3,2,1,0:T(1,128)} %refs_3_.1) | non-fusion elementwise | flops 2560 | bytes 15360
  1.4 4.5 %collective-permute-start.1 = (bf16[4,5,1,128]{3,2,1,0:T(2,128)(2,1)S(1)}, bf16[4,5,1,128]{3,2,1,0:T(2,128)(2,1)S(1)}, u32[]{:S(2)}, u32[]{:S(2)}) collective-permute-start(bf16[4,5,1,128]{3,2,1,0:T(2,128)(2,1)S(1)} %convert.19), channel_id=1, source_target_pairs={{4,0},{8,4},{12,8},{16,12},{20,16},{24,20},{28,24},{0,28},{5,1},{9... | collective-permute-start | bytes 15368 | tf_op jit(solution)/shard_map/ppermute | solution.py:307
  6.0 0.0 copy-done.1
  6.0 0.0 collective-permute-start
  6.0 1.3 %collective-permute-done.1 = bf16[4,5,1,128]{3,2,1,0:T(2,128)(2,1)S(1)} collective-permute-done((bf16[4,5,1,128]{3,2,1,0:T(2,128)(2,1)S(1)}, bf16[4,5,1,128]{3,2,1,0:T(2,128)(2,1)S(1)}, u32[]{:S(2)}, u32[]{:S(2)}) %collective-permute-start.1) | collective-permute-done | bytes 5152 | tf_op jit(solution)/shard_map/ppermute | solution.py:307
  7.4 3.5 %collective-permute-done = bf16[4,5,1,128]{3,1,2,0:T(8,128)(2,1)S(1)} collective-permute-done((bf16[4,5,1,128]{3,1,2,0:T(8,128)(2,1)S(1)}, bf16[4,5,1,128]{3,1,2,0:T(8,128)(2,1)S(1)}, u32[]{:S(2)}, u32[]{:S(2)}) %collective-permute-start) | collective-permute-done | bytes 5152 | tf_op jit(solution)/shard_map/ppermute | solution.py:306
  10.8 0.1 slice.19
  10.9 0.1 pad_maximum_fusion
  11.0 0.0 copy-done
  11.0 0.3 %fusion = f32[2,1,320]{2,1,0:T(1,128)S(1)} fusion(bf16[1,2,320,640]{3,2,1,0:T(8,128)(2,1)S(1)} %copy-done, bf16[2,640,1]{1,0,2:T(2,128)(2,1)S(1)} %bitcast.30), kind=kOutput, calls=%fused_computation | convolution fusion | flops 819200 | bytes 824320 | tf_op jit(solution)/shard_map/pij,pj->pi/dot_general | solution.py:311
  11.3 0.1 reshape.65
  11.4 0.0 copy-start.3
  11.4 0.0 copy-start.2
  11.4 0.1 reshape_reshape.3.precond_ref
  11.5 0.6 %copy-done.3 = f32[5,5,1,128]{3,2,1,0:T(1,128)S(1)} copy-done((f32[5,5,1,128]{3,2,1,0:T(1,128)S(1)}, f32[5,5,1,128]{3,2,1,0:T(1,128)}, u32[]{:S(2)}) %copy-start.3) | copy-done | bytes 12824
  12.2 0.0 copy-done.2
  12.2 1.0 %local.1 = (bf16[1344,128]{1,0:T(8,128)(2,1)}, f32[5,128]{1,0:T(8,128)S(1)}, f32[5,1,128]{2,1,0:T(1,128)}) custom-call(f32[5,128]{1,0:T(8,128)S(1)} %reshape_reshape.3.precond_ref, f32[4,5,1,128]{3,2,1,0:T(1,128)S(1)} %copy-done.1, f32[5,5,1,128]{3,2,1,0:T(1,128)S(1)} %copy-done.3, f32[4,5,1,128]{3,2,1,0:T(1,128)S(1)} %copy-done.2), custom_call_target="tpu_custom_call" | custom-call | tf_op jit(solution)/shard_map/local/pallas_call | solution.py:265
  13.2 2.8 %all-to-all-start = ((bf16[32,21,2,128]{3,2,1,0:T(2,128)(2,1)}), bf16[32,21,2,128]{3,2,1,0:T(2,128)(2,1)S(1)}, u32[]{:S(2)}, u32[]{:S(2)}) async-start(bf16[32,21,2,128]{3,2,1,0:T(2,128)(2,1)} %bitcast.28), calls=%async_computation | async-start | bytes 688128 | tf_op jit(solution)/shard_map/all_to_all | solution.py:294
  16.6 11.9 %all-to-all-done = bf16[32,21,2,128]{3,2,1,0:T(2,128)(2,1)S(1)} async-done(((bf16[32,21,2,128]{3,2,1,0:T(2,128)(2,1)}), bf16[32,21,2,128]{3,2,1,0:T(2,128)(2,1)S(1)}, u32[]{:S(2)}, u32[]{:S(2)}) %all-to-all-start) | async-done | bytes 344096 | tf_op jit(solution)/shard_map/all_to_all | solution.py:294
  28.6 1.0 %merged.1 = (f32[5,1,128]{2,1,0:T(1,128)}, f32[1,5]{1,0:T(1,128)}) custom-call(s32[1]{0:T(128)S(6)} %copy.23.refs_0_, f32[1344,128]{1,0:T(8,128)S(1)} %convert.13.refs_1_, f32[5,128]{1,0:T(8,128)S(1)} %get-tuple-element.10.refs_2_, f32[4,5,1,128]{3,2,1,0:T(1,128)S(1)} %copy-done.1, f32[4,5,1,128]{3,2,1,0:T(1,128)S(1)} %copy-done.2), custom_call_target="tpu_custom_call" | custom-call | tf_op jit(solution)/shard_map/merged/pallas_call | solution.py:278
  (10 shorter events, 0.1 us)
Async XLA Ops:
  0.6 10.4 %copy-start = (bf16[1,2,320,640]{3,2,1,0:T(8,128)(2,1)S(1)}, bf16[1,2,320,640]{3,2,1,0:T(8,128)(2,1)}, u32[]{:S(2)}) copy-start(bf16[1,2,320,640]{3,2,1,0:T(8,128)(2,1)} %param.8) | copy-start | bytes 2457604
  0.6 5.3 %copy-start.1 = (f32[4,5,1,128]{3,2,1,0:T(1,128)S(1)}, f32[4,5,1,128]{3,2,1,0:T(1,128)}, u32[]{:S(2)}) copy-start(f32[4,5,1,128]{3,2,1,0:T(1,128)} %refs_3_.1) | copy-start | bytes 30724
  1.4 5.9 %collective-permute-start.1 = (bf16[4,5,1,128]{3,2,1,0:T(2,128)(2,1)S(1)}, bf16[4,5,1,128]{3,2,1,0:T(2,128)(2,1)S(1)}, u32[]{:S(2)}, u32[]{:S(2)}) collective-permute-start(bf16[4,5,1,128]{3,2,1,0:T(2,128)(2,1)S(1)} %convert.19), channel_id=1, source_target_pairs={{4,0},{8,4},{12,8},{16,12},{20,16},{24,20},{28,24},{0,28},{5,1},{9... | collective-permute-start | bytes 15368 | tf_op jit(solution)/shard_map/ppermute | solution.py:307
  6.0 4.9 %collective-permute-start = (bf16[4,5,1,128]{3,1,2,0:T(8,128)(2,1)S(1)}, bf16[4,5,1,128]{3,1,2,0:T(8,128)(2,1)S(1)}, u32[]{:S(2)}, u32[]{:S(2)}) collective-permute-start(bf16[4,5,1,128]{3,1,2,0:T(8,128)(2,1)S(1)} %copy.9), channel_id=1, source_target_pairs={{0,4},{4,8},{8,12},{12,16},{16,20},{20,24},{24,28},{28,0},{1,5},{5... | collective-permute-start | bytes 15368 | tf_op jit(solution)/shard_map/ppermute | solution.py:306
  11.4 0.7 %copy-start.3 = (f32[5,5,1,128]{3,2,1,0:T(1,128)S(1)}, f32[5,5,1,128]{3,2,1,0:T(1,128)}, u32[]{:S(2)}) copy-start(f32[5,5,1,128]{3,2,1,0:T(1,128)} %jac_ref.1) | copy-start | bytes 38404
  11.4 0.7 %copy-start.2 = (f32[4,5,1,128]{3,2,1,0:T(1,128)S(1)}, f32[4,5,1,128]{3,2,1,0:T(1,128)}, u32[]{:S(2)}) copy-start(f32[4,5,1,128]{3,2,1,0:T(1,128)} %refs_4_.1) | copy-start | bytes 30724
  13.2 15.4 %all-to-all-start = ((bf16[32,21,2,128]{3,2,1,0:T(2,128)(2,1)}), bf16[32,21,2,128]{3,2,1,0:T(2,128)(2,1)S(1)}, u32[]{:S(2)}, u32[]{:S(2)}) async-start(bf16[32,21,2,128]{3,2,1,0:T(2,128)(2,1)} %bitcast.28), calls=%async_computation | async-start | bytes 688128 | tf_op jit(solution)/shard_map/all_to_all | solution.py:294

commit v4 on v3

--- a/solution.py
+++ b/solution.py
@@ -4,6 +4,7 @@
 from jax.experimental import pallas as pl
 from jax.experimental.pallas import tpu as pltpu
 from jax.sharding import PartitionSpec as P
+
 
 AXES = ("theta", "band")
 MERGED_LIMIT = 64
@@ -159,28 +160,69 @@
     return even((4 + kb) * ncomp + 1)
 
 
-def local_kernel(precond_ref, basis_ref, jac_ref, face_ref, send_ref, inner_ref, out_ref):
+def early_kernel(
+    basis_hbm, jac_hbm, face_hbm, panel_hbm, static_ref, sums_ref, block_ref, basis_ref, face_ref, panel_ref, jac_ref, sems
+):
+    pairs = ((basis_hbm, basis_ref), (jac_hbm, jac_ref), (face_hbm, face_ref), (panel_hbm, panel_ref))
+    copies = [pltpu.make_async_copy(source, target, sems.at[i]) for i, (source, target) in enumerate(pairs)]
+    for copy in copies:
+        copy.start()
+    for copy in copies[:3]:
+        copy.wait()
     kb, ncomp, _, width = basis_ref.shape
-    slot = message_rows(kb, ncomp)
-    precond = precond_ref[...]
-    out_ref[:, 0, :] = precond
-    lane = lax.broadcasted_iota(jnp.int32, (ncomp, width), 1)
-    lower = jnp.where(lane == 0, 0.0, pltpu.roll(precond, 1, 1))
-    upper = jnp.where(lane == width - 1, 0.0, pltpu.roll(precond, width - 1, 1))
-    inner = 6.0 * precond + coupled(jac_ref, precond)
-    inner = inner - (face_ref[0, :, 0, :] * lower + face_ref[1, :, 0, :] * upper)
-    inner_ref[...] = inner
     vectors = [basis_ref[i, :, 0, :] for i in range(kb)]
-    pairs = [vectors[i] * inner for i in range(kb)] + [inner * inner]
-    pairs += [vectors[i] * vectors[j] for i in range(kb) for j in range(kb)]
-    rows = jnp.concatenate(over_cells(pairs), axis=0)
+    pairs = [vectors[i] * vectors[j] for i in range(kb) for j in range(kb)]
+    blank = [jnp.zeros((1, width), jnp.float32)] * (kb + 1)
+    rows = jnp.concatenate(blank + over_cells(pairs), axis=0)
     high, middle, low = thirds(lane_reduced(rows))
     sums = high + pltpu.roll(middle, THIRD, 1) + pltpu.roll(low, 2 * THIRD, 1)
     row = lax.broadcasted_iota(jnp.int32, (ncomp, width), 0)
+    lane = lax.broadcasted_iota(jnp.int32, (ncomp, width), 1)
     first = jnp.where(lane == 3 * THIRD + row, face_ref[0, :, 0, :][:, :1], 0.0)
     last = jnp.where(lane == 3 * THIRD + THIRD // 2 + row, face_ref[1, :, 0, :][:, width - 1 :], 0.0)
-    sums += jnp.sum(first + last, axis=0, keepdims=True)
-    groups = [face_ref[2, :, 0, :], face_ref[3, :, 0, :], *vectors, inner, precond, sums]
+    sums_ref[...] = sums + jnp.sum(first + last, axis=0, keepdims=True)
+    static_ref[...] = jnp.concatenate([face_ref[2, :, 0, :], face_ref[3, :, 0, :], *vectors], axis=0)
+    for w in range(ncomp):
+        block_ref[w] = jac_ref[:, w, 0, :] + jnp.where(row == w, 6.0, 0.0)
+    copies[3].wait()
+
+
+def local_kernel(
+    before_ref, after_ref, panel_ref, basis_ref, face_ref, static_ref, sums_ref, block_ref, send_ref, inner_ref, out_ref
+):
+    kb, ncomp, _, width = basis_ref.shape
+    half = width // 2
+    slot = message_rows(kb, ncomp)
+    lane = lax.broadcasted_iota(jnp.int32, (ncomp, width), 1)
+    current = basis_ref[kb - 1, :, 0, :]
+    swapped = pltpu.roll(current, half, 1)
+    left = jnp.where(lane < half, pltpu.roll(before_ref[kb - 1, :, 0, :], half, 1), swapped)
+    right = jnp.where(lane < half, swapped, pltpu.roll(after_ref[kb - 1, :, 0, :], half, 1))
+    owned = []
+    for h, cells in enumerate((left, right)):
+        vector = jnp.concatenate([jnp.broadcast_to(cells[u : u + 1], (8, width)) for u in range(ncomp)], axis=1)
+        owned.append(
+            lax.dot_general(
+                vector.astype(jnp.bfloat16),
+                panel_ref[0, h],
+                (((1,), (1,)), ((), ())),
+                preferred_element_type=jnp.float32,
+            )[:1]
+        )
+    halves = [[owned[h][:, u * half : (u + 1) * half] for u in range(ncomp)] for h in range(2)]
+    precond = jnp.concatenate([jnp.concatenate([halves[0][u], halves[1][u]], axis=1) for u in range(ncomp)], axis=0)
+    out_ref[:, 0, :] = precond
+    lower = jnp.where(lane == 0, 0.0, pltpu.roll(precond, 1, 1))
+    upper = jnp.where(lane == width - 1, 0.0, pltpu.roll(precond, width - 1, 1))
+    inner = block_ref[0] * precond[0:1]
+    for w in range(1, ncomp):
+        inner += block_ref[w] * precond[w : w + 1]
+    inner = inner - (face_ref[0, :, 0, :] * lower + face_ref[1, :, 0, :] * upper)
+    inner_ref[...] = inner
+    pairs = [basis_ref[i, :, 0, :] * inner for i in range(kb)] + [inner * inner]
+    high, middle, low = thirds(lane_reduced(jnp.concatenate(over_cells(pairs), axis=0)))
+    sums = sums_ref[...] + high + pltpu.roll(middle, THIRD, 1) + pltpu.roll(low, 2 * THIRD, 1)
+    groups = [static_ref[...], inner, precond, sums]
     if slot > (4 + kb) * ncomp + 1:
         groups.append(jnp.zeros((slot - (4 + kb) * ncomp - 1, width), jnp.float32))
     message = jnp.concatenate(groups, axis=0).astype(jnp.bfloat16)
@@ -257,11 +299,27 @@
     finished(proj, gram, local[0, kb] + sums[0, kb], inner_ref[...] - outer, basis_ref, next_ref, hess_ref)
 
 
-def one_exchange(precond, basis, jac_block, face_coef, rotor_offset):
+def one_exchange(before, after, panel_inverse, basis, jac_block, face_coef, rotor_offset):
     kb, ncomp, _, width = basis.shape
     theta_count = lax.axis_size("theta")
     band_count = lax.axis_size("band")
     devices = theta_count * band_count
+    anywhere = pl.BlockSpec(memory_space=pl.ANY)
+    *early, basis, face_coef, panel_inverse = pl.pallas_call(
+        early_kernel,
+        out_shape=(
+            pltpu.VMEM(((2 + kb) * ncomp, width), jnp.float32),
+            pltpu.VMEM((1, width), jnp.float32),
+            pltpu.VMEM((ncomp, ncomp, width), jnp.float32),
+            pltpu.VMEM(basis.shape, basis.dtype),
+            pltpu.VMEM(face_coef.shape, face_coef.dtype),
+            pltpu.VMEM(panel_inverse.shape, panel_inverse.dtype),
+        ),
+        in_specs=[anywhere] * 4,
+        out_specs=specs(6),
+        scratch_shapes=[pltpu.VMEM(jac_block.shape, jac_block.dtype), pltpu.SemaphoreType.DMA((4,))],
+        name="early",
+    )(basis, jac_block, face_coef, panel_inverse)
     send, inner, precond = pl.pallas_call(
         local_kernel,
         out_shape=(
@@ -269,10 +327,10 @@
             pltpu.VMEM((ncomp, width), jnp.float32),
             jax.ShapeDtypeStruct((ncomp, 1, width), jnp.float32),
         ),
-        in_specs=specs(4),
+        in_specs=specs(8),
         out_specs=specs(3),
         name="local",
-    )(*in_vmem(precond.reshape(ncomp, width), basis, jac_block, face_coef))
+    )(*in_vmem(before, after, panel_inverse, basis, face_coef, *early))
     everyone = exchanged(send, devices)
     everyone = everyone.astype(jnp.float32)
     v_next, hess = pl.pallas_call(
@@ -300,20 +358,19 @@
     half = width // 2
     theta_count = lax.axis_size("theta")
     band_count = lax.axis_size("band")
-    merged = theta_count * band_count <= MERGED_LIMIT
     up = [(i, (i + 1) % theta_count) for i in range(theta_count)]
     down = [(j, i) for i, j in up]
     before = lax.ppermute(basis, "theta", up)
     after = lax.ppermute(basis, "theta", down)
+    if theta_count * band_count <= MERGED_LIMIT:
+        precond, v_next, hess = one_exchange(before, after, panel_inverse, basis, jac_block, face_coef, rotor_offset)
+        return precond, v_next, hess.reshape(kb + 1)
     before, current, after = (x[-1].astype(jnp.bfloat16) for x in (before, basis, after))
     extended = jnp.concatenate([before[..., half:], current, after[..., :half]], axis=2)
     panels = extended.reshape(ncomp, 2, width).transpose(1, 0, 2).reshape(2, ncomp * width)
     owned = jnp.einsum("pij,pj->pi", panel_inverse[0], panels, preferred_element_type=jnp.float32)
     precond = owned.reshape(2, ncomp, half).transpose(1, 0, 2).reshape(ncomp, 1, width)
-    if merged:
-        precond, v_next, hess = one_exchange(precond, basis, jac_block, face_coef, rotor_offset)
-    else:
-        v_next, hess = two_exchanges(precond, basis, jac_block, face_coef, rotor_offset)
+    v_next, hess = two_exchanges(precond, basis, jac_block, face_coef, rotor_offset)
     return precond, v_next, hess.reshape(kb + 1)
 
 

time: 30.1 us -> 28.6 us (0.950)
  waiting for transfers between devices: 16.8 us -> 12.3 us
  starting transfers between devices: 7.33 us -> 10.8 us
  Pallas kernels: 2.05 us -> 3.74 us
  local copies, waits for them, and re-layouts: 0.95 us -> 0 us
  other arithmetic: 0.91 us -> 0.05 us
  matrix products: 0.32 us -> 0 us
    all_to_all x1, starting transfers between devices: 2.81 us -> 6.19 us  [exchanged(): return lax.all_to_all(slots, AXES, 0, 0, tiled=True).reshape(rows.shape)]
    ppermute x1, waiting for transfers between devices: 3.48 us -> 0.27 us  [on_device(): before = lax.ppermute(basis, 'theta', up)]
    ppermute x1, waiting for transfers between devices: 1.35 us -> 0.09 us  [on_device(): after = lax.ppermute(basis, 'theta', down)]
    pallas_call x0 -> x1, Pallas kernels: none -> 1.23 us  [one_exchange(): pl.pallas_call(early_kernel, out_shape=(pltpu.VMEM(((2 + kb) * ncomp, wid...]
    unnamed x1 -> x0, other arithmetic: 0.79 us -> none
    unnamed x11 -> x0, local copies, waits for them, and re-layouts: 0.67 us -> none
    ppermute x1, starting transfers between devices: 0.01 us -> 0.55 us  [on_device(): before = lax.ppermute(basis, 'theta', up)]
    pallas_call x1, Pallas kernels: 1 us -> 1.46 us  [one_exchange(): pl.pallas_call(local_kernel, out_shape=(jax.ShapeDtypeStruct((devices * m...]
  transfers between devices with their start and end apart: 3 -> 3, of which waited for: 3 -> 3; matrix products, arithmetic and copies ran while one was open for 0% -> 0% of each run, Pallas kernels for 0% -> 4%
where the time goes in v4:
time: 28.6 us; the launch traced here: 28.2 us
  waiting for transfers between devices  12.3 us (43%)
  starting transfers between devices  10.8 us (38%)
  Pallas kernels  3.74 us (13%)
  between operations  1.3 us (5%)
    all_to_all x1, waiting for transfers between devices, exchanged(): return lax.all_to_all(slots, AXES, 0, 0, tiled=True).reshape(rows.shape)  11.9 us
    all_to_all x1, starting transfers between devices, exchanged(): return lax.all_to_all(slots, AXES, 0, 0, tiled=True).reshape(rows.shape)  6.19 us
    ppermute x1, starting transfers between devices, on_device(): after = lax.ppermute(basis, 'theta', down)  4.09 us
    pallas_call x1, Pallas kernels, one_exchange(): pl.pallas_call(local_kernel, out_shape=(jax.ShapeDtypeStruct((devices * m...  1.46 us
    pallas_call x1, Pallas kernels, one_exchange(): pl.pallas_call(early_kernel, out_shape=(pltpu.VMEM(((2 + kb) * ncomp, wid...  1.23 us
    pallas_call x1, Pallas kernels, one_exchange(): pl.pallas_call(lambda *refs: merged_kernel(theta_count, band_count, *refs...  1.05 us
  transfers between devices with their start and end apart: 3, of which 3 were waited for; matrix products, arithmetic and copies ran while one was open for 0% of the time, Pallas kernels for 4%

profile of v4, /device:TPU:0, one launch (start us, length us, event | category | flops | bytes accessed | tf_op | source)
XLA Modules:
  0.0 28.2 jit_solution(700915414969999201)
XLA Ops:
  0.6 0.5 %collective-permute-start = (f32[4,5,1,128]{3,2,1,0:T(1,128)}, f32[4,5,1,128]{3,2,1,0:T(1,128)S(1)}, u32[]{:S(2)}, u32[]{:S(2)}) collective-permute-start(f32[4,5,1,128]{3,2,1,0:T(1,128)} %basis_hbm.1), channel_id=1, source_target_pairs={{0,4},{4,8},{8,12},{12,16},{16,20},{20,24},{24,28},{28,0},{1,5},{5... | collective-permute-start | bytes 30728 | tf_op jit(solution)/shard_map/ppermute | solution.py:363
  1.2 4.1 %collective-permute-start.1 = (f32[4,5,1,128]{3,2,1,0:T(1,128)}, f32[4,5,1,128]{3,2,1,0:T(1,128)S(1)}, u32[]{:S(2)}, u32[]{:S(2)}) collective-permute-start(f32[4,5,1,128]{3,2,1,0:T(1,128)} %basis_hbm.1), channel_id=1, source_target_pairs={{4,0},{8,4},{12,8},{16,12},{20,16},{24,20},{28,24},{0,28},{5,1},{9... | collective-permute-start | bytes 30728 | tf_op jit(solution)/shard_map/ppermute | solution.py:364
  5.3 1.2 %early.1 = (f32[30,128]{1,0:T(8,128)S(1)}, f32[1,128]{1,0:T(1,128)S(1)}, f32[5,5,128]{2,1,0:T(8,128)S(1)}, f32[4,5,1,128]{3,2,1,0:T(1,128)S(1)}, f32[4,5,1,128]{...) custom-call(f32[4,5,1,128]{3,2,1,0:T(1,128)} %basis_hbm.1, f32[5,5,1,128]{3,2,1,0:T(1,128)} %jac_hbm.1, ...), custom_call_target="tpu_custom_call" | custom-call | tf_op jit(solution)/shard_map/early/pallas_call | solution.py:308
  6.5 0.3 collective-permute-done.before_ref
  6.8 0.1 collective-permute-done.1.after_ref
  6.9 1.5 %local.1 = (bf16[1344,128]{1,0:T(8,128)(2,1)}, f32[5,128]{1,0:T(8,128)S(1)}, f32[5,1,128]{2,1,0:T(1,128)}) custom-call(f32[4,5,1,128]{3,2,1,0:T(1,128)S(1)} %collective-permute-done.before_ref, f32[4,5,1,128]{3,2,1,0:T(1,128)S(1)} %collective-permute-done.1.after_ref, bf16[1,2,320,640]{3,2,1,0:T(8,128)(2,1)S(1)} %get-tuple-element.14.panel_ref, ...), custom_call_target="tpu_custom_call" | custom-call | tf_op jit(solution)/shard_map/local/pallas_call | solution.py:323
  8.3 6.2 %all-to-all-start = ((bf16[32,21,2,128]{3,2,1,0:T(2,128)(2,1)}), bf16[32,21,2,128]{3,2,1,0:T(2,128)(2,1)S(1)}, u32[]{:S(2)}, u32[]{:S(2)}) async-start(bf16[32,21,2,128]{3,2,1,0:T(2,128)(2,1)} %bitcast.5), calls=%async_computation | async-start | bytes 688128 | tf_op jit(solution)/shard_map/all_to_all | solution.py:352
  15.2 11.9 %all-to-all-done = bf16[32,21,2,128]{3,2,1,0:T(2,128)(2,1)S(1)} async-done(((bf16[32,21,2,128]{3,2,1,0:T(2,128)(2,1)}), bf16[32,21,2,128]{3,2,1,0:T(2,128)(2,1)S(1)}, u32[]{:S(2)}, u32[]{:S(2)}) %all-to-all-start) | async-done | bytes 344096 | tf_op jit(solution)/shard_map/all_to_all | solution.py:352
  27.2 1.0 %merged.1 = (f32[5,1,128]{2,1,0:T(1,128)}, f32[1,5]{1,0:T(1,128)}) custom-call(s32[1]{0:T(128)S(6)} %copy.8.refs_0_, f32[1344,128]{1,0:T(8,128)S(1)} %convert.1.refs_1_, f32[5,128]{1,0:T(8,128)S(1)} %get-tuple-element.22.refs_2_, f32[4,5,1,128]{3,2,1,0:T(1,128)S(1)} %get-tuple-element.15.basis_ref.refs_3_, ...), custom_call_target="tpu_custom_call" | custom-call | tf_op jit(solution)/shard_map/merged/pallas_call | solution.py:336
  (1 shorter events, 0.0 us)
Async XLA Ops:
  0.6 6.1 %collective-permute-start = (f32[4,5,1,128]{3,2,1,0:T(1,128)}, f32[4,5,1,128]{3,2,1,0:T(1,128)S(1)}, u32[]{:S(2)}, u32[]{:S(2)}) collective-permute-start(f32[4,5,1,128]{3,2,1,0:T(1,128)} %basis_hbm.1), channel_id=1, source_target_pairs={{0,4},{4,8},{8,12},{12,16},{16,20},{20,24},{24,28},{28,0},{1,5},{5... | collective-permute-start | bytes 30728 | tf_op jit(solution)/shard_map/ppermute | solution.py:363
  1.2 5.7 %collective-permute-start.1 = (f32[4,5,1,128]{3,2,1,0:T(1,128)}, f32[4,5,1,128]{3,2,1,0:T(1,128)S(1)}, u32[]{:S(2)}, u32[]{:S(2)}) collective-permute-start(f32[4,5,1,128]{3,2,1,0:T(1,128)} %basis_hbm.1), channel_id=1, source_target_pairs={{4,0},{8,4},{12,8},{16,12},{20,16},{24,20},{28,24},{0,28},{5,1},{9... | collective-permute-start | bytes 30728 | tf_op jit(solution)/shard_map/ppermute | solution.py:364
  8.3 18.8 %all-to-all-start = ((bf16[32,21,2,128]{3,2,1,0:T(2,128)(2,1)}), bf16[32,21,2,128]{3,2,1,0:T(2,128)(2,1)S(1)}, u32[]{:S(2)}, u32[]{:S(2)}) async-start(bf16[32,21,2,128]{3,2,1,0:T(2,128)(2,1)} %bitcast.5), calls=%async_computation | async-start | bytes 688128 | tf_op jit(solution)/shard_map/all_to_all | solution.py:352

commit v5 on v4

--- a/solution.py
+++ b/solution.py
@@ -161,7 +161,7 @@
 
 
 def early_kernel(
-    basis_hbm, jac_hbm, face_hbm, panel_hbm, static_ref, sums_ref, block_ref, basis_ref, face_ref, panel_ref, jac_ref, sems
+    offset_ref, basis_hbm, jac_hbm, face_hbm, panel_hbm, static_ref, sums_ref, block_ref, basis_ref, face_ref, panel_ref, jac_ref, sems
 ):
     pairs = ((basis_hbm, basis_ref), (jac_hbm, jac_ref), (face_hbm, face_ref), (panel_hbm, panel_ref))
     copies = [pltpu.make_async_copy(source, target, sems.at[i]) for i, (source, target) in enumerate(pairs)]
@@ -188,7 +188,7 @@
 
 
 def local_kernel(
-    before_ref, after_ref, panel_ref, basis_ref, face_ref, static_ref, sums_ref, block_ref, send_ref, inner_ref, out_ref
+    before_ref, after_ref, panel_ref, basis_ref, face_ref, static_ref, sums_ref, block_ref, send_ref, inner_ref, precond_ref
 ):
     kb, ncomp, _, width = basis_ref.shape
     half = width // 2
@@ -211,7 +211,7 @@
         )
     halves = [[owned[h][:, u * half : (u + 1) * half] for u in range(ncomp)] for h in range(2)]
     precond = jnp.concatenate([jnp.concatenate([halves[0][u], halves[1][u]], axis=1) for u in range(ncomp)], axis=0)
-    out_ref[:, 0, :] = precond
+    precond_ref[...] = precond
     lower = jnp.where(lane == 0, 0.0, pltpu.roll(precond, 1, 1))
     upper = jnp.where(lane == width - 1, 0.0, pltpu.roll(precond, width - 1, 1))
     inner = block_ref[0] * precond[0:1]
@@ -230,8 +230,9 @@
         send_ref[device * slot : (device + 1) * slot] = message
 
 
-def merged_kernel(theta_count, band_count, offset_ref, all_ref, inner_ref, basis_ref, face_ref, next_ref, hess_ref, own_ref):
+def merged_kernel(theta_count, band_count, offset_ref, all_ref, inner_ref, precond_ref, basis_ref, face_ref, out_ref, next_ref, hess_ref, own_ref):
     kb, ncomp, _, width = basis_ref.shape
+    out_ref[:, 0, :] = precond_ref[...]
     devices = theta_count * band_count
     cycle = theta_count * width
     total = ncomp * devices * width
@@ -315,17 +316,17 @@
             pltpu.VMEM(face_coef.shape, face_coef.dtype),
             pltpu.VMEM(panel_inverse.shape, panel_inverse.dtype),
         ),
-        in_specs=[anywhere] * 4,
+        in_specs=specs(0, 1) + [anywhere] * 4,
         out_specs=specs(6),
         scratch_shapes=[pltpu.VMEM(jac_block.shape, jac_block.dtype), pltpu.SemaphoreType.DMA((4,))],
         name="early",
-    )(basis, jac_block, face_coef, panel_inverse)
+    )(rotor_offset, basis, jac_block, face_coef, panel_inverse)
     send, inner, precond = pl.pallas_call(
         local_kernel,
         out_shape=(
-            jax.ShapeDtypeStruct((devices * message_rows(kb, ncomp), width), jnp.bfloat16),
+            pltpu.VMEM((devices * message_rows(kb, ncomp), width), jnp.bfloat16),
             pltpu.VMEM((ncomp, width), jnp.float32),
-            jax.ShapeDtypeStruct((ncomp, 1, width), jnp.float32),
+            pltpu.VMEM((ncomp, width), jnp.float32),
         ),
         in_specs=specs(8),
         out_specs=specs(3),
@@ -333,18 +334,18 @@
     )(*in_vmem(before, after, panel_inverse, basis, face_coef, *early))
     everyone = exchanged(send, devices)
     everyone = everyone.astype(jnp.float32)
-    v_next, hess = pl.pallas_call(
+    return pl.pallas_call(
         lambda *refs: merged_kernel(theta_count, band_count, *refs),
         out_shape=(
             jax.ShapeDtypeStruct((ncomp, 1, width), jnp.float32),
+            jax.ShapeDtypeStruct((ncomp, 1, width), jnp.float32),
             jax.ShapeDtypeStruct((1, kb + 1), jnp.float32),
         ),
-        in_specs=specs(4, 1),
-        out_specs=specs(2),
+        in_specs=specs(5, 1),
+        out_specs=specs(3),
         scratch_shapes=[pltpu.VMEM((3, ncomp, devices, width), jnp.float32)],
         name="merged",
-    )(rotor_offset, *in_vmem(everyone, inner, basis, face_coef))
-    return precond, v_next, hess
+    )(rotor_offset, *in_vmem(everyone, inner, precond, basis, face_coef))
 
 
 def exchanged(rows, devices):

time: 28.6 us -> 27.6 us (0.965)
  blocking collectives: 0 us -> 18.3 us
  waiting for transfers between devices: 12.3 us -> 0.01 us
  starting transfers between devices: 10.8 us -> 4.63 us
  Pallas kernels: 3.74 us -> 3.01 us
    all_to_all x0 -> x1, blocking collectives: none -> 18.3 us  [exchanged(): return lax.all_to_all(slots, AXES, 0, 0, tiled=True).reshape(rows.shape)]
    all_to_all x1 -> x0, waiting for transfers between devices: 11.9 us -> none  [exchanged(): return lax.all_to_all(slots, AXES, 0, 0, tiled=True).reshape(rows.shape)]
    all_to_all x1 -> x0, starting transfers between devices: 6.19 us -> none  [exchanged(): return lax.all_to_all(slots, AXES, 0, 0, tiled=True).reshape(rows.shape)]
    pallas_call x1, Pallas kernels: 1.46 us -> 0.72 us  [one_exchange(): pl.pallas_call(local_kernel, out_shape=(pltpu.VMEM((devices * message_row...]
  transfers between devices with their start and end apart: 3 -> 2, of which waited for: 3 -> 0; matrix products, arithmetic and copies ran while one was open for 0% -> 0% of each run, Pallas kernels for 4% -> 5%
where the time goes in v5:
time: 27.6 us; the launch traced here: 27.3 us
  blocking collectives  18.3 us (66%)
  starting transfers between devices  4.63 us (17%)
  Pallas kernels  3.01 us (11%)
  between operations  1.32 us (5%)
    all_to_all x1, blocking collectives, exchanged(): return lax.all_to_all(slots, AXES, 0, 0, tiled=True).reshape(rows.shape)  18.3 us
    ppermute x1, starting transfers between devices, on_device(): after = lax.ppermute(basis, 'theta', down)  4.09 us
    pallas_call x1, Pallas kernels, one_exchange(): pl.pallas_call(early_kernel, out_shape=(pltpu.VMEM(((2 + kb) * ncomp, wid...  1.23 us
    pallas_call x1, Pallas kernels, one_exchange(): pl.pallas_call(lambda *refs: merged_kernel(theta_count, band_count, *refs...  1.06 us
    pallas_call x1, Pallas kernels, one_exchange(): pl.pallas_call(local_kernel, out_shape=(pltpu.VMEM((devices * message_row...  0.72 us
  transfers between devices with their start and end apart: 2, of which 0 were waited for; matrix products, arithmetic and copies ran while one was open for 0% of the time, Pallas kernels for 5%

profile of v5, /device:TPU:0, one launch (start us, length us, event | category | flops | bytes accessed | tf_op | source)
XLA Modules:
  0.0 27.3 jit_solution(13917944074405776390)
XLA Ops:
  0.6 0.5 %collective-permute-start = (f32[4,5,1,128]{3,2,1,0:T(1,128)}, f32[4,5,1,128]{3,2,1,0:T(1,128)S(1)}, u32[]{:S(2)}, u32[]{:S(2)}) collective-permute-start(f32[4,5,1,128]{3,2,1,0:T(1,128)} %basis_hbm.1), channel_id=1, source_target_pairs={{0,4},{4,8},{8,12},{12,16},{16,20},{20,24},{24,28},{28,0},{1,5},{5... | collective-permute-start | bytes 30728 | tf_op jit(solution)/shard_map/ppermute | solution.py:364
  1.2 4.1 %collective-permute-start.1 = (f32[4,5,1,128]{3,2,1,0:T(1,128)}, f32[4,5,1,128]{3,2,1,0:T(1,128)S(1)}, u32[]{:S(2)}, u32[]{:S(2)}) collective-permute-start(f32[4,5,1,128]{3,2,1,0:T(1,128)} %basis_hbm.1), channel_id=1, source_target_pairs={{4,0},{8,4},{12,8},{16,12},{20,16},{24,20},{28,24},{0,28},{5,1},{9... | collective-permute-start | bytes 30728 | tf_op jit(solution)/shard_map/ppermute | solution.py:365
  5.9 1.2 %early.1 = (f32[30,128]{1,0:T(8,128)S(1)}, f32[1,128]{1,0:T(1,128)S(1)}, f32[5,5,128]{2,1,0:T(8,128)S(1)}, f32[4,5,1,128]{3,2,1,0:T(1,128)S(1)}, f32[4,5,1,128]{...) custom-call(s32[1]{0:T(128)S(6)} %copy.8.offset_ref.refs_0_, f32[4,5,1,128]{3,2,1,0:T(1,128)} %basis_hbm.1, ...), custom_call_target="tpu_custom_call" | custom-call | tf_op jit(solution)/shard_map/early/pallas_call | solution.py:309
  7.2 0.0 collective-permute-done.before_ref
  7.2 0.0 collective-permute-done.1.after_ref
  7.2 0.7 %local.1 = (bf16[1344,128]{1,0:T(8,128)(2,1)S(1)}, f32[5,128]{1,0:T(8,128)S(1)}, f32[5,128]{1,0:T(8,128)S(1)}) custom-call(f32[4,5,1,128]{3,2,1,0:T(1,128)S(1)} %collective-permute-done.before_ref, f32[4,5,1,128]{3,2,1,0:T(1,128)S(1)} %collective-permute-done.1.after_ref, bf16[1,2,320,640]{3,2,1,0:T(8,128)(2,1)S(1)} %get-tuple-element.15.panel_ref, ...), custom_call_target="tpu_custom_call" | custom-call | tf_op jit(solution)/shard_map/local/pallas_call | solution.py:324
  7.9 18.3 %all_to_all.5 = bf16[32,21,2,128]{3,2,1,0:T(2,128)(2,1)S(1)} all-to-all(bf16[32,21,2,128]{3,2,1,0:T(2,128)(2,1)S(1)} %bitcast.4), channel_id=1, replica_groups=mesh['theta'=8,'band'=4] {'theta','band'}, dimensions={0} | all-to-all | bytes 688128 | tf_op jit(solution)/shard_map/all_to_all | solution.py:353
  26.2 1.1 %merged.1 = (f32[5,1,128]{2,1,0:T(1,128)}, f32[5,1,128]{2,1,0:T(1,128)}, f32[1,5]{1,0:T(1,128)}) custom-call(s32[1]{0:T(128)S(6)} %copy.8.offset_ref.refs_0_, f32[1344,128]{1,0:T(8,128)S(1)} %convert.1.refs_1_, f32[5,128]{1,0:T(8,128)S(1)} %get-tuple-element.22.refs_2_, f32[5,128]{1,0:T(8,128)S(1)} %get-tuple-element.23.refs_3_, ...), custom_call_target="tpu_custom_call" | custom-call | tf_op jit(solution)/shard_map/merged/pallas_call | solution.py:337
  (1 shorter events, 0.0 us)
Async XLA Ops:
  0.6 6.5 %collective-permute-start = (f32[4,5,1,128]{3,2,1,0:T(1,128)}, f32[4,5,1,128]{3,2,1,0:T(1,128)S(1)}, u32[]{:S(2)}, u32[]{:S(2)}) collective-permute-start(f32[4,5,1,128]{3,2,1,0:T(1,128)} %basis_hbm.1), channel_id=1, source_target_pairs={{0,4},{4,8},{8,12},{12,16},{16,20},{20,24},{24,28},{28,0},{1,5},{5... | collective-permute-start | bytes 30728 | tf_op jit(solution)/shard_map/ppermute | solution.py:364
  1.2 6.0 %collective-permute-start.1 = (f32[4,5,1,128]{3,2,1,0:T(1,128)}, f32[4,5,1,128]{3,2,1,0:T(1,128)S(1)}, u32[]{:S(2)}, u32[]{:S(2)}) collective-permute-start(f32[4,5,1,128]{3,2,1,0:T(1,128)} %basis_hbm.1), channel_id=1, source_target_pairs={{4,0},{8,4},{12,8},{16,12},{20,16},{24,20},{28,24},{0,28},{5,1},{9... | collective-permute-start | bytes 30728 | tf_op jit(solution)/shard_map/ppermute | solution.py:365

commit v6 on v5

--- a/solution.py
+++ b/solution.py
@@ -9,6 +9,7 @@
 AXES = ("theta", "band")
 MERGED_LIMIT = 64
 THIRD = 32
+EIGHT = 8
 
 
 def even(count):
@@ -156,14 +157,28 @@
     return high, middle, x - high - middle
 
 
+def shared_pairs(kb, ncomp):
+    pairs = [(i, u) for i in range(kb) for u in range(ncomp)]
+    count = -(-(kb + 1) * ncomp // 2)
+    return pairs[:count], pairs[count:]
+
+
 def message_rows(kb, ncomp):
-    return even((4 + kb) * ncomp + 1)
+    return even(3 * ncomp + 2 + len(shared_pairs(kb, ncomp)[0]))
+
+
+def places(base, array):
+    row = lax.broadcasted_iota(jnp.int32, array.shape, 0)
+    lane = lax.broadcasted_iota(jnp.int32, array.shape, 1)
+    width = array.shape[1]
+    out = jnp.where(lane == base + row, array[:, :1], 0.0)
+    return out + jnp.where(lane == base + width // 2 + row, array[:, width - 1 :], 0.0)
 
 
 def early_kernel(
-    offset_ref, basis_hbm, jac_hbm, face_hbm, panel_hbm, static_ref, sums_ref, block_ref, basis_ref, face_ref, panel_ref, jac_ref, sems
+    basis_hbm, jac_hbm, face_hbm, panel_hbm, offset_hbm, sums_ref, edge_ref, block_ref, basis_ref, face_ref, panel_ref, offset_ref, jac_ref, sems
 ):
-    pairs = ((basis_hbm, basis_ref), (jac_hbm, jac_ref), (face_hbm, face_ref), (panel_hbm, panel_ref))
+    pairs = ((basis_hbm, basis_ref), (jac_hbm, jac_ref), (face_hbm, face_ref), (panel_hbm, panel_ref), (offset_hbm, offset_ref))
     copies = [pltpu.make_async_copy(source, target, sems.at[i]) for i, (source, target) in enumerate(pairs)]
     for copy in copies:
         copy.start()
@@ -175,20 +190,32 @@
     blank = [jnp.zeros((1, width), jnp.float32)] * (kb + 1)
     rows = jnp.concatenate(blank + over_cells(pairs), axis=0)
     high, middle, low = thirds(lane_reduced(rows))
-    sums = high + pltpu.roll(middle, THIRD, 1) + pltpu.roll(low, 2 * THIRD, 1)
+    sums_ref[...] = high + pltpu.roll(middle, THIRD, 1) + pltpu.roll(low, 2 * THIRD, 1)
     row = lax.broadcasted_iota(jnp.int32, (ncomp, width), 0)
     lane = lax.broadcasted_iota(jnp.int32, (ncomp, width), 1)
-    first = jnp.where(lane == 3 * THIRD + row, face_ref[0, :, 0, :][:, :1], 0.0)
-    last = jnp.where(lane == 3 * THIRD + THIRD // 2 + row, face_ref[1, :, 0, :][:, width - 1 :], 0.0)
-    sums_ref[...] = sums + jnp.sum(first + last, axis=0, keepdims=True)
-    static_ref[...] = jnp.concatenate([face_ref[2, :, 0, :], face_ref[3, :, 0, :], *vectors], axis=0)
+    edges = jnp.where(lane < width // 2, face_ref[0, :, 0, :], face_ref[1, :, 0, :])
+    edge = sum(places(EIGHT * i, array) for i, array in enumerate([edges, *vectors]))
+    edge_ref[...] = jnp.sum(edge, axis=0, keepdims=True)
     for w in range(ncomp):
         block_ref[w] = jac_ref[:, w, 0, :] + jnp.where(row == w, 6.0, 0.0)
     copies[3].wait()
+    copies[4].wait()
 
 
 def local_kernel(
-    before_ref, after_ref, panel_ref, basis_ref, face_ref, static_ref, sums_ref, block_ref, send_ref, inner_ref, precond_ref
+    before_ref,
+    after_ref,
+    far_basis_ref,
+    far_face_ref,
+    panel_ref,
+    basis_ref,
+    face_ref,
+    sums_ref,
+    edge_ref,
+    block_ref,
+    send_ref,
+    inner_ref,
+    precond_ref,
 ):
     kb, ncomp, _, width = basis_ref.shape
     half = width // 2
@@ -219,12 +246,24 @@
         inner += block_ref[w] * precond[w : w + 1]
     inner = inner - (face_ref[0, :, 0, :] * lower + face_ref[1, :, 0, :] * upper)
     inner_ref[...] = inner
-    pairs = [basis_ref[i, :, 0, :] * inner for i in range(kb)] + [inner * inner]
+    band = lax.axis_index("band")
+    is_even = lax.rem(band, 2) == 0
+    beside = jnp.logical_or(band == 1, band == 2)
+    lower_face, upper_face = face_ref[2, :, 0, :], face_ref[3, :, 0, :]
+    to_partner = jnp.where(is_even, upper_face, lower_face)
+    to_rotor = jnp.where(is_even, lower_face, upper_face)
+    reach = jnp.where(is_even, far_face_ref[2, :, 0, :], far_face_ref[3, :, 0, :]) * precond
+    pairs = [basis_ref[i, :, 0, :] * inner - far_basis_ref[i, :, 0, :] * reach for i in range(kb)] + [inner * inner]
     high, middle, low = thirds(lane_reduced(jnp.concatenate(over_cells(pairs), axis=0)))
     sums = sums_ref[...] + high + pltpu.roll(middle, THIRD, 1) + pltpu.roll(low, 2 * THIRD, 1)
-    groups = [static_ref[...], inner, precond, sums]
-    if slot > (4 + kb) * ncomp + 1:
-        groups.append(jnp.zeros((slot - (4 + kb) * ncomp - 1, width), jnp.float32))
+    carried, kept = shared_pairs(kb, ncomp)
+    for_partner = jnp.concatenate([far_basis_ref[i, u : u + 1, 0, :] for i, u in carried], axis=0)
+    spare = [jnp.zeros((1, width), jnp.float32)] * (len(carried) - ncomp - len(kept))
+    own_part = jnp.concatenate([to_rotor] + [basis_ref[i, u : u + 1, 0, :] for i, u in kept] + spare, axis=0)
+    groups = [to_partner, inner, precond, sums, edge_ref[...], jnp.where(beside, own_part, for_partner)]
+    filled = 3 * ncomp + 2 + len(carried)
+    if slot > filled:
+        groups.append(jnp.zeros((slot - filled, width), jnp.float32))
     message = jnp.concatenate(groups, axis=0).astype(jnp.bfloat16)
     for device in range(send_ref.shape[0] // slot):
         send_ref[device * slot : (device + 1) * slot] = message
@@ -254,11 +293,15 @@
         return pltpu.roll(x, (devices - count) % devices, 0)
 
     half = theta_count // 2
-    local = part((4 + kb) * ncomp)
+    is_even = lax.rem(band, 2) == 0
+    beside = jnp.logical_or(band == middle - 1, band == middle)
+    local, edge_row = part(3 * ncomp), part(3 * ncomp + 1)
+    tail = 3 * ncomp + 2
     square = jnp.zeros(shape, jnp.float32)
-    cross = [jnp.zeros(shape, jnp.float32) for _ in range(kb)]
+    at_edges = jnp.zeros(shape, jnp.float32)
+    turns, handed = [], []
     for u in range(ncomp):
-        inner, precond = part((2 + kb) * ncomp + u), part((3 + kb) * ncomp + u)
+        inner, precond = part(ncomp + u), part(2 * ncomp + u)
         turned = pltpu.roll(precond, lax.rem(width - skip, width), 1)
         near, at, far = (rows_up(turned, (half + k) * band_count + 1) for k in (-1, 0, 1))
         split = lane < width - skip
@@ -267,24 +310,39 @@
         near, at, far = (rows_up(turned, (-half + k) * band_count - 1) for k in (1, 0, -1))
         split = lane >= skip
         rotor_down = jnp.where(split, jnp.where(late, at, near), jnp.where(late, far, at))
-        band_plus = jnp.where(band == middle - 1, rotor_up, rows_up(precond, 1))
-        band_plus = jnp.where(band == band_count - 1, 0.0, band_plus)
-        band_minus = jnp.where(band == middle, rotor_down, rows_up(precond, -1))
-        band_minus = jnp.where(band == 0, 0.0, band_minus)
+        rotor = jnp.where(band == middle - 1, rotor_up, jnp.where(band == middle, rotor_down, 0.0))
+        partner = jnp.where(is_even, rows_up(precond, 1), rows_up(precond, -1))
         before = rows_up(pltpu.roll(precond, 1, 1), -band_count)
         after = rows_up(pltpu.roll(precond, width - 1, 1), band_count)
         edge = jnp.where(lane == 0, before, after)
-        place = 3 * THIRD + u
-        first = pltpu.roll(local, width - place, 1)
-        last = pltpu.roll(local, width - 1 - place - THIRD // 2, 1)
+        first = pltpu.roll(edge_row, (width - u) % width, 1)
+        last = pltpu.roll(edge_row, width - 1 - width // 2 - u, 1)
         coef = jnp.where(lane == 0, first, jnp.where(lane == width - 1, last, 0.0))
-        own_ref[0, u] = band_minus
-        own_ref[1, u] = band_plus
+        own_ref[0, u] = partner
+        own_ref[1, u] = rotor
         own_ref[2, u] = edge
-        outer = part(u) * band_minus + part(ncomp + u) * band_plus + coef * edge
+        rim = coef * edge
+        turn = part(tail + u) * rotor
+        turns.append(turn)
+        handed.append(jnp.where(is_even, rows_up(turn, 1), rows_up(turn, -1)))
+        outer = part(u) * partner + turn + rim
         square += outer * (outer - 2.0 * inner)
-        for i in range(kb):
-            cross[i] += part((2 + i) * ncomp + u) * outer
+        at_edges = jnp.where(lane == u, pltpu.roll(rim, u, 1), at_edges)
+        at_edges = jnp.where(lane == width // 2 + u, pltpu.roll(rim, width // 2 + 1 + u, 1), at_edges)
+    carried, kept = shared_pairs(kb, ncomp)
+    cross = [pltpu.roll(edge_row, width - EIGHT * (i + 1), 1) * at_edges for i in range(kb)]
+    in_partner = [jnp.zeros(shape, jnp.float32) for _ in range(kb)]
+    in_own = [jnp.zeros(shape, jnp.float32) for _ in range(kb)]
+    for place, (i, u) in enumerate(carried):
+        values = handed[u]
+        mine = place - ncomp
+        if 0 <= mine < len(kept):
+            values = jnp.where(beside, turns[kept[mine][1]], values)
+        product = part(tail + place) * values
+        in_partner[i] += product
+        if 0 <= mine < len(kept):
+            in_own[kept[mine][0]] += product
+    cross = [cross[i] + jnp.where(beside, in_own[i], in_partner[i]) for i in range(kb)]
     local = jnp.sum(local, axis=0, keepdims=True) / total
     local = local + pltpu.roll(local, width - THIRD, 1) + pltpu.roll(local, width - 2 * THIRD, 1)
     sums = lane_reduced(jnp.concatenate(over_cells(cross + [square]), axis=0)) / total
@@ -296,31 +354,35 @@
 
     lane = lax.broadcasted_iota(jnp.int32, (ncomp, width), 1)
     edges = jnp.where(lane == 0, face_ref[0, :, 0, :], jnp.where(lane == width - 1, face_ref[1, :, 0, :], 0.0))
-    outer = face_ref[2, :, 0, :] * own(0) + face_ref[3, :, 0, :] * own(1) + edges * own(2)
+    is_even = lax.rem(lax.axis_index("band"), 2) == 0
+    lower_face, upper_face = face_ref[2, :, 0, :], face_ref[3, :, 0, :]
+    outer = jnp.where(is_even, upper_face, lower_face) * own(0) + edges * own(2)
+    outer += jnp.where(is_even, lower_face, upper_face) * own(1)
     finished(proj, gram, local[0, kb] + sums[0, kb], inner_ref[...] - outer, basis_ref, next_ref, hess_ref)
 
 
-def one_exchange(before, after, panel_inverse, basis, jac_block, face_coef, rotor_offset):
+def one_exchange(before, after, far, panel_inverse, basis, jac_block, face_coef, rotor_offset):
     kb, ncomp, _, width = basis.shape
     theta_count = lax.axis_size("theta")
     band_count = lax.axis_size("band")
     devices = theta_count * band_count
     anywhere = pl.BlockSpec(memory_space=pl.ANY)
-    *early, basis, face_coef, panel_inverse = pl.pallas_call(
+    *early, basis, face_coef, panel_inverse, rotor_offset = pl.pallas_call(
         early_kernel,
         out_shape=(
-            pltpu.VMEM(((2 + kb) * ncomp, width), jnp.float32),
+            pltpu.VMEM((1, width), jnp.float32),
             pltpu.VMEM((1, width), jnp.float32),
             pltpu.VMEM((ncomp, ncomp, width), jnp.float32),
             pltpu.VMEM(basis.shape, basis.dtype),
             pltpu.VMEM(face_coef.shape, face_coef.dtype),
             pltpu.VMEM(panel_inverse.shape, panel_inverse.dtype),
+            pltpu.SMEM(rotor_offset.shape, rotor_offset.dtype),
         ),
-        in_specs=specs(0, 1) + [anywhere] * 4,
-        out_specs=specs(6),
-        scratch_shapes=[pltpu.VMEM(jac_block.shape, jac_block.dtype), pltpu.SemaphoreType.DMA((4,))],
+        in_specs=[anywhere] * 5,
+        out_specs=specs(6) + specs(0, 1),
+        scratch_shapes=[pltpu.VMEM(jac_block.shape, jac_block.dtype), pltpu.SemaphoreType.DMA((5,))],
         name="early",
-    )(rotor_offset, basis, jac_block, face_coef, panel_inverse)
+    )(basis, jac_block, face_coef, panel_inverse, rotor_offset)
     send, inner, precond = pl.pallas_call(
         local_kernel,
         out_shape=(
@@ -328,10 +390,10 @@
             pltpu.VMEM((ncomp, width), jnp.float32),
             pltpu.VMEM((ncomp, width), jnp.float32),
         ),
-        in_specs=specs(8),
+        in_specs=specs(10),
         out_specs=specs(3),
         name="local",
-    )(*in_vmem(before, after, panel_inverse, basis, face_coef, *early))
+    )(*in_vmem(before, after, *far, panel_inverse, basis, face_coef, *early))
     everyone = exchanged(send, devices)
     everyone = everyone.astype(jnp.float32)
     return pl.pallas_call(
@@ -363,8 +425,11 @@
     down = [(j, i) for i, j in up]
     before = lax.ppermute(basis, "theta", up)
     after = lax.ppermute(basis, "theta", down)
-    if theta_count * band_count <= MERGED_LIMIT:
-        precond, v_next, hess = one_exchange(before, after, panel_inverse, basis, jac_block, face_coef, rotor_offset)
+    if theta_count * band_count <= MERGED_LIMIT and band_count == 4:
+        pairs = [(b, b + 1 - 2 * (b % 2)) for b in range(band_count)]
+        far_basis = lax.ppermute(basis, "band", pairs)
+        far = [far_basis, lax.ppermute(face_coef, "band", pairs)]
+        precond, v_next, hess = one_exchange(before, after, far, panel_inverse, basis, jac_block, face_coef, rotor_offset)
         return precond, v_next, hess.reshape(kb + 1)
     before, current, after = (x[-1].astype(jnp.bfloat16) for x in (before, basis, after))
     extended = jnp.concatenate([before[..., half:], current, after[..., :half]], axis=2)

time: 27.6 us -> 27.3 us (0.989)
  blocking collectives: 18.3 us -> 16 us
  starting transfers between devices: 4.63 us -> 6.58 us
    ppermute x0 -> x2, starting transfers between devices: none -> 3.17 us  [the longest x1 3.03 us: on_device(): far = [far_basis, lax.ppermute(face_coef, 'band', pairs)]]
    all_to_all x1, blocking collectives: 18.3 us -> 16 us  [exchanged(): return lax.all_to_all(slots, AXES, 0, 0, tiled=True).reshape(rows.shape)]
    ppermute x1, starting transfers between devices: 4.09 us -> 3.4 us  [on_device(): after = lax.ppermute(basis, 'theta', down)]
    ppermute x1, starting transfers between devices: 0.54 us -> 0.01 us  [on_device(): before = lax.ppermute(basis, 'theta', up)]
  transfers between devices with their start and end apart: 2 -> 4, of which waited for: 0 -> 0; matrix products, arithmetic and copies ran while one was open for 0% -> 0% of each run, Pallas kernels for 5% -> 5%
where the time goes in v6:
time: 27.3 us; the launch traced here: 27.1 us
  blocking collectives  16 us (59%)
  starting transfers between devices  6.58 us (24%)
  Pallas kernels  3.09 us (11%)
  between operations  1.34 us (5%)
    all_to_all x1, blocking collectives, exchanged(): return lax.all_to_all(slots, AXES, 0, 0, tiled=True).reshape(rows.shape)  16 us
    ppermute x1, starting transfers between devices, on_device(): after = lax.ppermute(basis, 'theta', down)  3.4 us
    ppermute x1, starting transfers between devices, on_device(): far = [far_basis, lax.ppermute(face_coef, 'band', pairs)]  3.03 us
    pallas_call x1, Pallas kernels, one_exchange(): pl.pallas_call(early_kernel, out_shape=(pltpu.VMEM((1, width), jnp.float3...  1.25 us
    pallas_call x1, Pallas kernels, one_exchange(): pl.pallas_call(lambda *refs: merged_kernel(theta_count, band_count, *refs...  1.11 us
    pallas_call x1, Pallas kernels, one_exchange(): pl.pallas_call(local_kernel, out_shape=(pltpu.VMEM((devices * message_row...  0.73 us
  transfers between devices with their start and end apart: 4, of which 0 were waited for; matrix products, arithmetic and copies ran while one was open for 0% of the time, Pallas kernels for 5%

profile of v6, /device:TPU:0, one launch (start us, length us, event | category | flops | bytes accessed | tf_op | source)
XLA Modules:
  0.0 27.1 jit_solution(9782942151174249022)
XLA Ops:
  0.6 3.0 %collective-permute-start.3 = (f32[4,5,1,128]{3,2,1,0:T(1,128)}, f32[4,5,1,128]{3,2,1,0:T(1,128)S(1)}, u32[]{:S(2)}, u32[]{:S(2)}) collective-permute-start(f32[4,5,1,128]{3,2,1,0:T(1,128)} %face_hbm.1), channel_id=1, source_target_pairs={{0,1},{1,0},{2,3},{3,2},{4,5},{5,4},{6,7},{7,6},{8,9},{9,8},{10,11... | collective-permute-start | bytes 30728 | tf_op jit(solution)/shard_map/ppermute | solution.py:431
  3.7 0.0 collective-permute-start
  3.7 0.1 collective-permute-start.2
  3.8 3.4 %collective-permute-start.1 = (f32[4,5,1,128]{3,2,1,0:T(1,128)}, f32[4,5,1,128]{3,2,1,0:T(1,128)S(1)}, u32[]{:S(2)}, u32[]{:S(2)}) collective-permute-start(f32[4,5,1,128]{3,2,1,0:T(1,128)} %basis_hbm.1), channel_id=1, source_target_pairs={{4,0},{8,4},{12,8},{16,12},{20,16},{24,20},{28,24},{0,28},{5,1},{9... | collective-permute-start | bytes 30728 | tf_op jit(solution)/shard_map/ppermute | solution.py:427
  7.9 1.2 %early.1 = (f32[1,128]{1,0:T(1,128)S(1)}, f32[1,128]{1,0:T(1,128)S(1)}, f32[5,5,128]{2,1,0:T(8,128)S(1)}, f32[4,5,1,128]{3,2,1,0:T(1,128)S(1)}, f32[4,5,1,128]{3...) custom-call(f32[4,5,1,128]{3,2,1,0:T(1,128)} %basis_hbm.1, f32[5,5,1,128]{3,2,1,0:T(1,128)} %jac_hbm.1, ...), custom_call_target="tpu_custom_call" | custom-call | tf_op jit(solution)/shard_map/early/pallas_call | solution.py:370
  9.1 0.0 collective-permute-done.3.far_face_ref
  9.1 0.0 collective-permute-done.before_ref
  9.1 0.0 collective-permute-done.2.far_basis_ref
  9.2 0.0 collective-permute-done.1.after_ref
  9.2 0.7 %local.1 = (bf16[960,128]{1,0:T(8,128)(2,1)S(1)}, f32[5,128]{1,0:T(8,128)S(1)}, f32[5,128]{1,0:T(8,128)S(1)}) custom-call(f32[4,5,1,128]{3,2,1,0:T(1,128)S(1)} %collective-permute-done.before_ref, f32[4,5,1,128]{3,2,1,0:T(1,128)S(1)} %collective-permute-done.1.after_ref, f32[4,5,1,128]{3,2,1,0:T(1,128)S(1)} %collective-permute-done.2.far_basis_ref, ...), custom_call_target="tpu_custom_call" | custom-call | tf_op jit(solution)/shard_map/local/pallas_call | solution.py:386
  9.9 16.0 %all_to_all.5 = bf16[32,15,2,128]{3,2,1,0:T(2,128)(2,1)S(1)} all-to-all(bf16[32,15,2,128]{3,2,1,0:T(2,128)(2,1)S(1)} %bitcast.4), channel_id=1, replica_groups=mesh['theta'=8,'band'=4] {'theta','band'}, dimensions={0} | all-to-all | bytes 491520 | tf_op jit(solution)/shard_map/all_to_all | solution.py:415
  26.0 1.1 %merged.1 = (f32[5,1,128]{2,1,0:T(1,128)}, f32[5,1,128]{2,1,0:T(1,128)}, f32[1,5]{1,0:T(1,128)}) custom-call(s32[1]{0:T(128)S(4)} %get-tuple-element.16.refs_0_, f32[960,128]{1,0:T(8,128)S(1)} %convert.1.refs_1_, f32[5,128]{1,0:T(8,128)S(1)} %get-tuple-element.24.refs_2_, f32[5,128]{1,0:T(8,128)S(1)} %get-tuple-element.25.refs_3_, ...), custom_call_target="tpu_custom_call" | custom-call | tf_op jit(solution)/shard_map/merged/pallas_call | solution.py:399
  (1 shorter events, 0.0 us)
Async XLA Ops:
  0.6 8.5 %collective-permute-start.3 = (f32[4,5,1,128]{3,2,1,0:T(1,128)}, f32[4,5,1,128]{3,2,1,0:T(1,128)S(1)}, u32[]{:S(2)}, u32[]{:S(2)}) collective-permute-start(f32[4,5,1,128]{3,2,1,0:T(1,128)} %face_hbm.1), channel_id=1, source_target_pairs={{0,1},{1,0},{2,3},{3,2},{4,5},{5,4},{6,7},{7,6},{8,9},{9,8},{10,11... | collective-permute-start | bytes 30728 | tf_op jit(solution)/shard_map/ppermute | solution.py:431
  3.7 5.5 %collective-permute-start = (f32[4,5,1,128]{3,2,1,0:T(1,128)}, f32[4,5,1,128]{3,2,1,0:T(1,128)S(1)}, u32[]{:S(2)}, u32[]{:S(2)}) collective-permute-start(f32[4,5,1,128]{3,2,1,0:T(1,128)} %basis_hbm.1), channel_id=1, source_target_pairs={{0,4},{4,8},{8,12},{12,16},{16,20},{20,24},{24,28},{28,0},{1,5},{5... | collective-permute-start | bytes 30728 | tf_op jit(solution)/shard_map/ppermute | solution.py:426
  3.7 5.5 %collective-permute-start.2 = (f32[4,5,1,128]{3,2,1,0:T(1,128)}, f32[4,5,1,128]{3,2,1,0:T(1,128)S(1)}, u32[]{:S(2)}, u32[]{:S(2)}) collective-permute-start(f32[4,5,1,128]{3,2,1,0:T(1,128)} %basis_hbm.1), channel_id=1, source_target_pairs={{0,1},{1,0},{2,3},{3,2},{4,5},{5,4},{6,7},{7,6},{8,9},{9,8},{10,11... | collective-permute-start | bytes 30728 | tf_op jit(solution)/shard_map/ppermute | solution.py:430
  3.8 5.3 %collective-permute-start.1 = (f32[4,5,1,128]{3,2,1,0:T(1,128)}, f32[4,5,1,128]{3,2,1,0:T(1,128)S(1)}, u32[]{:S(2)}, u32[]{:S(2)}) collective-permute-start(f32[4,5,1,128]{3,2,1,0:T(1,128)} %basis_hbm.1), channel_id=1, source_target_pairs={{4,0},{8,4},{12,8},{16,12},{20,16},{24,20},{28,24},{0,28},{5,1},{9... | collective-permute-start | bytes 30728 | tf_op jit(solution)/shard_map/ppermute | solution.py:427

commit v7 on v6

--- a/solution.py
+++ b/solution.py
@@ -203,8 +203,8 @@
 
 
 def local_kernel(
-    before_ref,
-    after_ref,
+    near_ref,
+    beyond_ref,
     far_basis_ref,
     far_face_ref,
     panel_ref,
@@ -223,8 +223,10 @@
     lane = lax.broadcasted_iota(jnp.int32, (ncomp, width), 1)
     current = basis_ref[kb - 1, :, 0, :]
     swapped = pltpu.roll(current, half, 1)
-    left = jnp.where(lane < half, pltpu.roll(before_ref[kb - 1, :, 0, :], half, 1), swapped)
-    right = jnp.where(lane < half, swapped, pltpu.roll(after_ref[kb - 1, :, 0, :], half, 1))
+    near, beyond = near_ref[kb - 1, :, 0, :], beyond_ref[kb - 1, :, 0, :]
+    is_low = lax.rem(lax.axis_index("theta"), 2) == 0
+    left = jnp.where(lane < half, pltpu.roll(jnp.where(is_low, beyond, near), half, 1), swapped)
+    right = jnp.where(lane < half, swapped, pltpu.roll(jnp.where(is_low, near, beyond), half, 1))
     owned = []
     for h, cells in enumerate((left, right)):
         vector = jnp.concatenate([jnp.broadcast_to(cells[u : u + 1], (8, width)) for u in range(ncomp)], axis=1)
@@ -361,7 +363,7 @@
     finished(proj, gram, local[0, kb] + sums[0, kb], inner_ref[...] - outer, basis_ref, next_ref, hess_ref)
 
 
-def one_exchange(before, after, far, panel_inverse, basis, jac_block, face_coef, rotor_offset):
+def one_exchange(near, beyond, far, panel_inverse, basis, jac_block, face_coef, rotor_offset):
     kb, ncomp, _, width = basis.shape
     theta_count = lax.axis_size("theta")
     band_count = lax.axis_size("band")
@@ -393,7 +395,7 @@
         in_specs=specs(10),
         out_specs=specs(3),
         name="local",
-    )(*in_vmem(before, after, *far, panel_inverse, basis, face_coef, *early))
+    )(*in_vmem(near, beyond, *far, panel_inverse, basis, face_coef, *early))
     everyone = exchanged(send, devices)
     everyone = everyone.astype(jnp.float32)
     return pl.pallas_call(
@@ -423,14 +425,17 @@
     band_count = lax.axis_size("band")
     up = [(i, (i + 1) % theta_count) for i in range(theta_count)]
     down = [(j, i) for i, j in up]
-    before = lax.ppermute(basis, "theta", up)
-    after = lax.ppermute(basis, "theta", down)
-    if theta_count * band_count <= MERGED_LIMIT and band_count == 4:
+    if theta_count * band_count <= MERGED_LIMIT and band_count == 4 and theta_count % 2 == 0:
         pairs = [(b, b + 1 - 2 * (b % 2)) for b in range(band_count)]
         far_basis = lax.ppermute(basis, "band", pairs)
         far = [far_basis, lax.ppermute(face_coef, "band", pairs)]
-        precond, v_next, hess = one_exchange(before, after, far, panel_inverse, basis, jac_block, face_coef, rotor_offset)
+        near = lax.ppermute(basis, "theta", [(t, t + 1 - 2 * (t % 2)) for t in range(theta_count)])
+        turned = [(t, (t - 1 + 2 * (t % 2)) % theta_count) for t in range(theta_count)]
+        beyond = lax.ppermute(basis, "theta", turned)
+        precond, v_next, hess = one_exchange(near, beyond, far, panel_inverse, basis, jac_block, face_coef, rotor_offset)
         return precond, v_next, hess.reshape(kb + 1)
+    before = lax.ppermute(basis, "theta", up)
+    after = lax.ppermute(basis, "theta", down)
     before, current, after = (x[-1].astype(jnp.bfloat16) for x in (before, basis, after))
     extended = jnp.concatenate([before[..., half:], current, after[..., :half]], axis=2)
     panels = extended.reshape(ncomp, 2, width).transpose(1, 0, 2).reshape(2, ncomp * width)

time: 27.3 us -> 27.5 us (level)
  starting transfers between devices: 6.58 us -> 7 us
    ppermute x2, starting transfers between devices: 3.41 us -> 3.82 us  [the longest x1 3.82 us: on_device(): beyond = lax.ppermute(basis, 'theta', turned)]
where the time goes in v7:
time: 27.5 us; the launch traced here: 27.3 us
  blocking collectives  15.8 us (57%)
  starting transfers between devices  7 us (25%)
  Pallas kernels  3.1 us (11%)
  between operations  1.34 us (5%)
    all_to_all x1, blocking collectives, exchanged(): return lax.all_to_all(slots, AXES, 0, 0, tiled=True).reshape(rows.shape)  15.8 us
    ppermute x1, starting transfers between devices, on_device(): beyond = lax.ppermute(basis, 'theta', turned)  3.82 us
    ppermute x1, starting transfers between devices, on_device(): far = [far_basis, lax.ppermute(face_coef, 'band', pairs)]  3.03 us
    pallas_call x1, Pallas kernels, one_exchange(): pl.pallas_call(early_kernel, out_shape=(pltpu.VMEM((1, width), jnp.float3...  1.25 us
    pallas_call x1, Pallas kernels, one_exchange(): pl.pallas_call(lambda *refs: merged_kernel(theta_count, band_count, *refs...  1.11 us
    pallas_call x1, Pallas kernels, one_exchange(): pl.pallas_call(local_kernel, out_shape=(pltpu.VMEM((devices * message_row...  0.74 us
  transfers between devices with their start and end apart: 4, of which 0 were waited for; matrix products, arithmetic and copies ran while one was open for 0% of the time, Pallas kernels for 5%

profile of v7, /device:TPU:0, one launch (start us, length us, event | category | flops | bytes accessed | tf_op | source)
XLA Modules:
  0.0 27.3 jit_solution(8826027428901583732)
XLA Ops:
  0.6 3.0 %collective-permute-start.3 = (f32[4,5,1,128]{3,2,1,0:T(1,128)}, f32[4,5,1,128]{3,2,1,0:T(1,128)S(1)}, u32[]{:S(2)}, u32[]{:S(2)}) collective-permute-start(f32[4,5,1,128]{3,2,1,0:T(1,128)} %face_hbm.1), channel_id=1, source_target_pairs={{0,1},{1,0},{2,3},{3,2},{4,5},{5,4},{6,7},{7,6},{8,9},{9,8},{10,11... | collective-permute-start | bytes 30728 | tf_op jit(solution)/shard_map/ppermute | solution.py:431
  3.7 0.0 collective-permute-start
  3.7 0.2 collective-permute-start.2
  3.8 3.8 %collective-permute-start.1 = (f32[4,5,1,128]{3,2,1,0:T(1,128)}, f32[4,5,1,128]{3,2,1,0:T(1,128)S(1)}, u32[]{:S(2)}, u32[]{:S(2)}) collective-permute-start(f32[4,5,1,128]{3,2,1,0:T(1,128)} %basis_hbm.1), channel_id=1, source_target_pairs={{0,28},{4,8},{8,4},{12,16},{16,12},{20,24},{24,20},{28,0},{1,29},{... | collective-permute-start | bytes 30728 | tf_op jit(solution)/shard_map/ppermute | solution.py:434
  8.3 1.2 %early.1 = (f32[1,128]{1,0:T(1,128)S(1)}, f32[1,128]{1,0:T(1,128)S(1)}, f32[5,5,128]{2,1,0:T(8,128)S(1)}, f32[4,5,1,128]{3,2,1,0:T(1,128)S(1)}, f32[4,5,1,128]{3...) custom-call(f32[4,5,1,128]{3,2,1,0:T(1,128)} %basis_hbm.1, f32[5,5,1,128]{3,2,1,0:T(1,128)} %jac_hbm.1, ...), custom_call_target="tpu_custom_call" | custom-call | tf_op jit(solution)/shard_map/early/pallas_call | solution.py:372
  9.5 0.0 collective-permute-done.3.far_face_ref
  9.6 0.0 collective-permute-done.near_ref
  9.6 0.0 collective-permute-done.2.far_basis_ref
  9.6 0.0 collective-permute-done.1.beyond_ref
  9.6 0.7 %local.1 = (bf16[960,128]{1,0:T(8,128)(2,1)S(1)}, f32[5,128]{1,0:T(8,128)S(1)}, f32[5,128]{1,0:T(8,128)S(1)}) custom-call(f32[4,5,1,128]{3,2,1,0:T(1,128)S(1)} %collective-permute-done.near_ref, f32[4,5,1,128]{3,2,1,0:T(1,128)S(1)} %collective-permute-done.1.beyond_ref, f32[4,5,1,128]{3,2,1,0:T(1,128)S(1)} %collective-permute-done.2.far_basis_ref, ...), custom_call_target="tpu_custom_call" | custom-call | tf_op jit(solution)/shard_map/local/pallas_call | solution.py:388
  10.3 15.8 %all_to_all.5 = bf16[32,15,2,128]{3,2,1,0:T(2,128)(2,1)S(1)} all-to-all(bf16[32,15,2,128]{3,2,1,0:T(2,128)(2,1)S(1)} %bitcast.4), channel_id=1, replica_groups=mesh['theta'=8,'band'=4] {'theta','band'}, dimensions={0} | all-to-all | bytes 491520 | tf_op jit(solution)/shard_map/all_to_all | solution.py:417
  26.2 1.1 %merged.1 = (f32[5,1,128]{2,1,0:T(1,128)}, f32[5,1,128]{2,1,0:T(1,128)}, f32[1,5]{1,0:T(1,128)}) custom-call(s32[1]{0:T(128)S(4)} %get-tuple-element.16.refs_0_, f32[960,128]{1,0:T(8,128)S(1)} %convert.1.refs_1_, f32[5,128]{1,0:T(8,128)S(1)} %get-tuple-element.24.refs_2_, f32[5,128]{1,0:T(8,128)S(1)} %get-tuple-element.25.refs_3_, ...), custom_call_target="tpu_custom_call" | custom-call | tf_op jit(solution)/shard_map/merged/pallas_call | solution.py:401
  (1 shorter events, 0.0 us)
Async XLA Ops:
  0.6 8.9 %collective-permute-start.3 = (f32[4,5,1,128]{3,2,1,0:T(1,128)}, f32[4,5,1,128]{3,2,1,0:T(1,128)S(1)}, u32[]{:S(2)}, u32[]{:S(2)}) collective-permute-start(f32[4,5,1,128]{3,2,1,0:T(1,128)} %face_hbm.1), channel_id=1, source_target_pairs={{0,1},{1,0},{2,3},{3,2},{4,5},{5,4},{6,7},{7,6},{8,9},{9,8},{10,11... | collective-permute-start | bytes 30728 | tf_op jit(solution)/shard_map/ppermute | solution.py:431
  3.7 5.9 %collective-permute-start = (f32[4,5,1,128]{3,2,1,0:T(1,128)}, f32[4,5,1,128]{3,2,1,0:T(1,128)S(1)}, u32[]{:S(2)}, u32[]{:S(2)}) collective-permute-start(f32[4,5,1,128]{3,2,1,0:T(1,128)} %basis_hbm.1), channel_id=1, source_target_pairs={{0,4},{4,0},{8,12},{12,8},{16,20},{20,16},{24,28},{28,24},{1,5},{5... | collective-permute-start | bytes 30728 | tf_op jit(solution)/shard_map/ppermute | solution.py:432
  3.7 5.9 %collective-permute-start.2 = (f32[4,5,1,128]{3,2,1,0:T(1,128)}, f32[4,5,1,128]{3,2,1,0:T(1,128)S(1)}, u32[]{:S(2)}, u32[]{:S(2)}) collective-permute-start(f32[4,5,1,128]{3,2,1,0:T(1,128)} %basis_hbm.1), channel_id=1, source_target_pairs={{0,1},{1,0},{2,3},{3,2},{4,5},{5,4},{6,7},{7,6},{8,9},{9,8},{10,11... | collective-permute-start | bytes 30728 | tf_op jit(solution)/shard_map/ppermute | solution.py:430
  3.8 5.8 %collective-permute-start.1 = (f32[4,5,1,128]{3,2,1,0:T(1,128)}, f32[4,5,1,128]{3,2,1,0:T(1,128)S(1)}, u32[]{:S(2)}, u32[]{:S(2)}) collective-permute-start(f32[4,5,1,128]{3,2,1,0:T(1,128)} %basis_hbm.1), channel_id=1, source_target_pairs={{0,28},{4,8},{8,4},{12,16},{16,12},{20,24},{24,20},{28,0},{1,29},{... | collective-permute-start | bytes 30728 | tf_op jit(solution)/shard_map/ppermute | solution.py:434

commit v8 on v7

--- a/solution.py
+++ b/solution.py
@@ -8,8 +8,6 @@
 
 AXES = ("theta", "band")
 MERGED_LIMIT = 64
-THIRD = 32
-EIGHT = 8
 
 
 def even(count):
@@ -45,25 +43,24 @@
     return [jnp.sum(array, axis=0, keepdims=True) for array in arrays]
 
 
-def finished(proj, gram, square, image, basis_ref, next_ref, hess_ref):
+def finished(sums, image, basis_ref, next_ref, hess_ref):
     kb = basis_ref.shape[0]
-    squares = square
+    lane = lax.broadcasted_iota(jnp.int32, sums.shape, 1)
+    proj = [sums[:, i : i + 1] for i in range(kb)]
+    left, right = jnp.zeros_like(sums), jnp.zeros_like(sums)
     for i in range(kb):
-        squares -= 2.0 * proj[i] * proj[i]
-    for i in range(kb):
-        for j in range(kb):
-            squares += proj[i] * gram[i * kb + j] * proj[j]
+        first = kb + 1 + i * kb
+        left = jnp.where(jnp.logical_and(lane >= first, lane < first + kb), proj[i], left)
+        column = jnp.logical_and(lane > kb, lax.rem(lane - kb - 1, kb) == i)
+        right = jnp.where(column, proj[i], right)
+    terms = jnp.where(lane < kb, -2.0 * sums * sums, jnp.where(lane == kb, sums, left * right * sums))
+    squares = jnp.sum(terms, axis=1, keepdims=True)
     drop = proj[0] * basis_ref[0, :, 0, :]
     for i in range(1, kb):
         drop += proj[i] * basis_ref[i, :, 0, :]
-    row = (1, image.shape[1])
-    hnorm = jnp.sqrt(jnp.full(row, squares + 1e-06, jnp.float32))
+    hnorm = jnp.sqrt(jnp.broadcast_to(squares + 1e-06, sums.shape))
     next_ref[:, 0, :] = (image - drop) / hnorm
-    lane = lax.broadcasted_iota(jnp.int32, row, 1)
-    hess = hnorm
-    for i in range(kb):
-        hess = jnp.where(lane == i, proj[i], hess)
-    hess_ref[...] = hess[:, : kb + 1]
+    hess_ref[...] = jnp.where(lane < kb, sums, hnorm)[:, : kb + 1]
 
 
 def image_kernel(theta_count, band_count, offset_ref, all_ref, basis_ref, jac_ref, face_ref, image_ref, send_ref):
@@ -116,11 +113,8 @@
 
 
 def finish_kernel(total, sums_ref, image_ref, basis_ref, next_ref, hess_ref):
-    kb = basis_ref.shape[0]
     sums = jnp.sum(sums_ref[...], axis=0, keepdims=True) / total
-    proj = [sums[0, i] for i in range(kb)]
-    gram = [sums[0, kb + 1 + i] for i in range(kb * kb)]
-    finished(proj, gram, sums[0, kb], image_ref[...], basis_ref, next_ref, hess_ref)
+    finished(sums, image_ref[...], basis_ref, next_ref, hess_ref)
 
 
 def two_exchanges(precond, basis, jac_block, face_coef, rotor_offset):
@@ -151,20 +145,23 @@
     )(*in_vmem(sums, image, basis))
 
 
-def thirds(x):
-    high = x.astype(jnp.bfloat16).astype(jnp.float32)
-    middle = (x - high).astype(jnp.bfloat16).astype(jnp.float32)
-    return high, middle, x - high - middle
+def sums_lane(kb, ncomp):
+    return (kb + 3) * ncomp
+
+
+def spread(sums, lane):
+    high = sums.astype(jnp.bfloat16).astype(jnp.float32)
+    return pltpu.roll(high, lane, 1) + pltpu.roll(sums - high, lane + sums.shape[1] // 2, 1)
 
 
 def shared_pairs(kb, ncomp):
     pairs = [(i, u) for i in range(kb) for u in range(ncomp)]
-    count = -(-(kb + 1) * ncomp // 2)
+    count = -(-(kb + 2) * ncomp // 2)
     return pairs[:count], pairs[count:]
 
 
 def message_rows(kb, ncomp):
-    return even(3 * ncomp + 2 + len(shared_pairs(kb, ncomp)[0]))
+    return even(2 * ncomp + 1 + len(shared_pairs(kb, ncomp)[0]))
 
 
 def places(base, array):
@@ -176,7 +173,7 @@
 
 
 def early_kernel(
-    basis_hbm, jac_hbm, face_hbm, panel_hbm, offset_hbm, sums_ref, edge_ref, block_ref, basis_ref, face_ref, panel_ref, offset_ref, jac_ref, sems
+    basis_hbm, jac_hbm, face_hbm, panel_hbm, offset_hbm, ready_ref, block_ref, basis_ref, face_ref, panel_ref, offset_ref, jac_ref, sems
 ):
     pairs = ((basis_hbm, basis_ref), (jac_hbm, jac_ref), (face_hbm, face_ref), (panel_hbm, panel_ref), (offset_hbm, offset_ref))
     copies = [pltpu.make_async_copy(source, target, sems.at[i]) for i, (source, target) in enumerate(pairs)]
@@ -189,13 +186,14 @@
     pairs = [vectors[i] * vectors[j] for i in range(kb) for j in range(kb)]
     blank = [jnp.zeros((1, width), jnp.float32)] * (kb + 1)
     rows = jnp.concatenate(blank + over_cells(pairs), axis=0)
-    high, middle, low = thirds(lane_reduced(rows))
-    sums_ref[...] = high + pltpu.roll(middle, THIRD, 1) + pltpu.roll(low, 2 * THIRD, 1)
+    sums = spread(lane_reduced(rows), sums_lane(kb, ncomp))
     row = lax.broadcasted_iota(jnp.int32, (ncomp, width), 0)
     lane = lax.broadcasted_iota(jnp.int32, (ncomp, width), 1)
     edges = jnp.where(lane < width // 2, face_ref[0, :, 0, :], face_ref[1, :, 0, :])
-    edge = sum(places(EIGHT * i, array) for i, array in enumerate([edges, *vectors]))
-    edge_ref[...] = jnp.sum(edge, axis=0, keepdims=True)
+    edge = sum(places(ncomp * i, array) for i, array in enumerate([edges, *vectors]))
+    is_even = lax.rem(lax.axis_index("band"), 2) == 0
+    edge += places(ncomp * (kb + 2), jnp.where(is_even, face_ref[3, :, 0, :], face_ref[2, :, 0, :]))
+    ready_ref[...] = sums + jnp.sum(edge, axis=0, keepdims=True)
     for w in range(ncomp):
         block_ref[w] = jac_ref[:, w, 0, :] + jnp.where(row == w, 6.0, 0.0)
     copies[3].wait()
@@ -210,8 +208,7 @@
     panel_ref,
     basis_ref,
     face_ref,
-    sums_ref,
-    edge_ref,
+    ready_ref,
     block_ref,
     send_ref,
     inner_ref,
@@ -255,15 +252,18 @@
     to_partner = jnp.where(is_even, upper_face, lower_face)
     to_rotor = jnp.where(is_even, lower_face, upper_face)
     reach = jnp.where(is_even, far_face_ref[2, :, 0, :], far_face_ref[3, :, 0, :]) * precond
-    pairs = [basis_ref[i, :, 0, :] * inner - far_basis_ref[i, :, 0, :] * reach for i in range(kb)] + [inner * inner]
-    high, middle, low = thirds(lane_reduced(jnp.concatenate(over_cells(pairs), axis=0)))
-    sums = sums_ref[...] + high + pltpu.roll(middle, THIRD, 1) + pltpu.roll(low, 2 * THIRD, 1)
+    pairs = [basis_ref[i, :, 0, :] * inner - far_basis_ref[i, :, 0, :] * reach for i in range(kb)]
+    pairs.append(inner * inner + jnp.where(beside, reach * reach, 0.0))
+    sums = spread(lane_reduced(jnp.concatenate(over_cells(pairs), axis=0)), sums_lane(kb, ncomp))
+    edge = ready_ref[...] + sums + jnp.sum(places(ncomp * (kb + 1), inner), axis=0, keepdims=True)
     carried, kept = shared_pairs(kb, ncomp)
     for_partner = jnp.concatenate([far_basis_ref[i, u : u + 1, 0, :] for i, u in carried], axis=0)
-    spare = [jnp.zeros((1, width), jnp.float32)] * (len(carried) - ncomp - len(kept))
-    own_part = jnp.concatenate([to_rotor] + [basis_ref[i, u : u + 1, 0, :] for i, u in kept] + spare, axis=0)
-    groups = [to_partner, inner, precond, sums, edge_ref[...], jnp.where(beside, own_part, for_partner)]
-    filled = 3 * ncomp + 2 + len(carried)
+    spare = [jnp.zeros((1, width), jnp.float32)] * (len(carried) - 2 * ncomp - len(kept))
+    kept_rows = [basis_ref[i, u : u + 1, 0, :] for i, u in kept]
+    own_part = jnp.concatenate([to_partner, to_rotor, *kept_rows, *spare], axis=0)
+    head = inner * jnp.where(beside, 1.0, to_partner)
+    groups = [head, precond, edge, jnp.where(beside, own_part, for_partner)]
+    filled = 2 * ncomp + 1 + len(carried)
     if slot > filled:
         groups.append(jnp.zeros((slot - filled, width), jnp.float32))
     message = jnp.concatenate(groups, axis=0).astype(jnp.bfloat16)
@@ -271,96 +271,103 @@
         send_ref[device * slot : (device + 1) * slot] = message
 
 
-def merged_kernel(theta_count, band_count, offset_ref, all_ref, inner_ref, precond_ref, basis_ref, face_ref, out_ref, next_ref, hess_ref, own_ref):
+def merged_kernel(
+    theta_count, band_count, offset_ref, all_ref, inner_ref, precond_ref, basis_ref, face_ref, out_ref, next_ref, hess_ref, own_ref
+):
     kb, ncomp, _, width = basis_ref.shape
     out_ref[:, 0, :] = precond_ref[...]
-    devices = theta_count * band_count
-    cycle = theta_count * width
-    total = ncomp * devices * width
+    total = ncomp * theta_count * band_count * width
+    slot = all_ref.shape[0] // (theta_count * band_count)
     middle = band_count // 2
-    shape = (devices, width)
-    row = lax.broadcasted_iota(jnp.int32, shape, 0)
+    half = theta_count // 2
+    side = width // 2
+    tail = 2 * ncomp + 1
+    bands = range(band_count)
+    shape = (theta_count, width)
     lane = lax.broadcasted_iota(jnp.int32, shape, 1)
-    band = lax.rem(row, band_count)
-    here = lax.axis_index("theta") * band_count + lax.axis_index("band")
-    base = cycle // 2 - width
-    start = offset_ref[0] - base
+    start = offset_ref[0] - (theta_count // 2 - 1) * width
     late = start >= width
     skip = jnp.where(late, start - width, start)
-
-    def part(place):
-        return all_ref[pl.ds(place, devices, stride=all_ref.shape[0] // devices), :]
-
-    def rows_up(x, count):
-        return pltpu.roll(x, (devices - count) % devices, 0)
-
-    half = theta_count // 2
+    back = lax.rem(width - skip, width)
+
+    def part(band, place):
+        return all_ref[pl.ds(band * slot + place, theta_count, stride=band_count * slot), :]
+
+    def around(x, count):
+        return pltpu.roll(x, -count % theta_count, 0)
+
+    edge_rows = [part(b, 2 * ncomp) for b in bands]
+    zero = jnp.zeros(shape, jnp.float32)
+    square = zero
+    below, above, gap = [zero] * band_count, [zero] * band_count, [zero] * band_count
+    turns = {middle - 1: [], middle: []}
+    for u in range(ncomp):
+        precond = [part(b, ncomp + u) for b in bands]
+        turned = pltpu.roll(precond[middle], back, 1)
+        first = jnp.where(late, around(turned, half), around(turned, half - 1))
+        rotor_up = jnp.where(lane < width - skip, first, around(first, 1))
+        turned = pltpu.roll(precond[middle - 1], skip, 1)
+        first = jnp.where(late, around(turned, -half), around(turned, 1 - half))
+        rotor = {middle - 1: rotor_up, middle: jnp.where(lane >= skip, first, around(first, -1))}
+        for b in bands:
+            partner = precond[b + 1 - 2 * (b % 2)]
+            own_ref[0, u, b * theta_count : (b + 1) * theta_count] = partner
+            head = part(b, u)
+            if b in rotor:
+                own_ref[1, u, b * theta_count : (b + 1) * theta_count] = rotor[b]
+                turns[b].append(part(b, tail + ncomp + u) * rotor[b])
+                outer = part(b, tail + u) * partner + turns[b][u]
+                square += outer * (outer - 2.0 * head)
+                distance = outer - head
+                gap[b] = jnp.where(lane == u, pltpu.roll(distance, u, 1), gap[b])
+                gap[b] = jnp.where(lane == side + u, pltpu.roll(distance, side + 1 + u, 1), gap[b])
+            else:
+                square -= 2.0 * head * partner
+            below[b] = jnp.where(lane == u, pltpu.roll(precond[b], u + 1, 1), below[b])
+            above[b] = jnp.where(lane == side + u, pltpu.roll(precond[b], side + u, 1), above[b])
+    cross = [zero] * kb
+    carried, kept = shared_pairs(kb, ncomp)
+    for b in bands:
+        crossing = jnp.where(lane < side, around(below[b], -1), around(above[b], 1))
+        if b not in turns:
+            other = b + 1 - 2 * (b % 2)
+            ends = pltpu.roll(jnp.where(lane < side, below[other], above[other]), side, 1)
+            gap[b] = pltpu.roll(edge_rows[b], width - ncomp * (kb + 2), 1) * ends
+            gap[b] -= pltpu.roll(edge_rows[b], width - ncomp * (kb + 1), 1)
+        own_ref[2, 0, b * theta_count : (b + 1) * theta_count] = crossing
+        rim = jnp.where(lax.rem(lane, side) < ncomp, edge_rows[b] * crossing, 0.0)
+        square += rim * (rim + 2.0 * gap[b])
+        for i in range(kb):
+            cross[i] += pltpu.roll(edge_rows[b], width - ncomp * (i + 1), 1) * rim
+    for b, turn in turns.items():
+        for place, (i, u) in enumerate(carried):
+            cross[i] += part(b + 1 - 2 * (b % 2), tail + place) * turn[u]
+        for place, (i, u) in enumerate(kept):
+            cross[i] += part(b, tail + 2 * ncomp + place) * turn[u]
+    local = jnp.sum(sum(edge_rows), axis=0, keepdims=True) / total
+    at = sums_lane(kb, ncomp)
+    local = pltpu.roll(local, width - at, 1) + pltpu.roll(local, side - at, 1)
+    sums = lane_reduced(jnp.concatenate(over_cells(cross + [square]), axis=0)) / total
+    place = lax.broadcasted_iota(jnp.int32, sums.shape, 1)
+    sums = local + jnp.where(place < kb, -sums, jnp.where(place == kb, sums, 0.0))
+
+    theta, band = lax.axis_index("theta"), lax.axis_index("band")
+    here = band * theta_count + theta
+    cells = (ncomp, width)
+    lane = lax.broadcasted_iota(jnp.int32, cells, 1)
+    row = lax.broadcasted_iota(jnp.int32, cells, 0)
+    crossing = own_ref[2, 0, pl.ds(here, 1), :]
+    lowest = jnp.sum(jnp.where(lane == row, crossing, 0.0), axis=1, keepdims=True)
+    highest = jnp.sum(jnp.where(lane == side + row, crossing, 0.0), axis=1, keepdims=True)
+    outer = jnp.where(lane == 0, face_ref[0, :, 0, :] * lowest, 0.0)
+    outer += jnp.where(lane == width - 1, face_ref[1, :, 0, :] * highest, 0.0)
     is_even = lax.rem(band, 2) == 0
     beside = jnp.logical_or(band == middle - 1, band == middle)
-    local, edge_row = part(3 * ncomp), part(3 * ncomp + 1)
-    tail = 3 * ncomp + 2
-    square = jnp.zeros(shape, jnp.float32)
-    at_edges = jnp.zeros(shape, jnp.float32)
-    turns, handed = [], []
-    for u in range(ncomp):
-        inner, precond = part(ncomp + u), part(2 * ncomp + u)
-        turned = pltpu.roll(precond, lax.rem(width - skip, width), 1)
-        near, at, far = (rows_up(turned, (half + k) * band_count + 1) for k in (-1, 0, 1))
-        split = lane < width - skip
-        rotor_up = jnp.where(split, jnp.where(late, at, near), jnp.where(late, far, at))
-        turned = pltpu.roll(precond, skip, 1)
-        near, at, far = (rows_up(turned, (-half + k) * band_count - 1) for k in (1, 0, -1))
-        split = lane >= skip
-        rotor_down = jnp.where(split, jnp.where(late, at, near), jnp.where(late, far, at))
-        rotor = jnp.where(band == middle - 1, rotor_up, jnp.where(band == middle, rotor_down, 0.0))
-        partner = jnp.where(is_even, rows_up(precond, 1), rows_up(precond, -1))
-        before = rows_up(pltpu.roll(precond, 1, 1), -band_count)
-        after = rows_up(pltpu.roll(precond, width - 1, 1), band_count)
-        edge = jnp.where(lane == 0, before, after)
-        first = pltpu.roll(edge_row, (width - u) % width, 1)
-        last = pltpu.roll(edge_row, width - 1 - width // 2 - u, 1)
-        coef = jnp.where(lane == 0, first, jnp.where(lane == width - 1, last, 0.0))
-        own_ref[0, u] = partner
-        own_ref[1, u] = rotor
-        own_ref[2, u] = edge
-        rim = coef * edge
-        turn = part(tail + u) * rotor
-        turns.append(turn)
-        handed.append(jnp.where(is_even, rows_up(turn, 1), rows_up(turn, -1)))
-        outer = part(u) * partner + turn + rim
-        square += outer * (outer - 2.0 * inner)
-        at_edges = jnp.where(lane == u, pltpu.roll(rim, u, 1), at_edges)
-        at_edges = jnp.where(lane == width // 2 + u, pltpu.roll(rim, width // 2 + 1 + u, 1), at_edges)
-    carried, kept = shared_pairs(kb, ncomp)
-    cross = [pltpu.roll(edge_row, width - EIGHT * (i + 1), 1) * at_edges for i in range(kb)]
-    in_partner = [jnp.zeros(shape, jnp.float32) for _ in range(kb)]
-    in_own = [jnp.zeros(shape, jnp.float32) for _ in range(kb)]
-    for place, (i, u) in enumerate(carried):
-        values = handed[u]
-        mine = place - ncomp
-        if 0 <= mine < len(kept):
-            values = jnp.where(beside, turns[kept[mine][1]], values)
-        product = part(tail + place) * values
-        in_partner[i] += product
-        if 0 <= mine < len(kept):
-            in_own[kept[mine][0]] += product
-    cross = [cross[i] + jnp.where(beside, in_own[i], in_partner[i]) for i in range(kb)]
-    local = jnp.sum(local, axis=0, keepdims=True) / total
-    local = local + pltpu.roll(local, width - THIRD, 1) + pltpu.roll(local, width - 2 * THIRD, 1)
-    sums = lane_reduced(jnp.concatenate(over_cells(cross + [square]), axis=0)) / total
-    proj = [local[0, i] - sums[0, i] for i in range(kb)]
-    gram = [local[0, kb + 1 + i] for i in range(kb * kb)]
-
-    def own(k):
-        return own_ref[k, :, pl.ds(here, 1), :].reshape(ncomp, width)
-
-    lane = lax.broadcasted_iota(jnp.int32, (ncomp, width), 1)
-    edges = jnp.where(lane == 0, face_ref[0, :, 0, :], jnp.where(lane == width - 1, face_ref[1, :, 0, :], 0.0))
-    is_even = lax.rem(lax.axis_index("band"), 2) == 0
     lower_face, upper_face = face_ref[2, :, 0, :], face_ref[3, :, 0, :]
-    outer = jnp.where(is_even, upper_face, lower_face) * own(0) + edges * own(2)
-    outer += jnp.where(is_even, lower_face, upper_face) * own(1)
-    finished(proj, gram, local[0, kb] + sums[0, kb], inner_ref[...] - outer, basis_ref, next_ref, hess_ref)
+    outer += jnp.where(is_even, upper_face, lower_face) * own_ref[0, :, pl.ds(here, 1), :].reshape(cells)
+    rotor = jnp.where(is_even, lower_face, upper_face) * own_ref[1, :, pl.ds(here, 1), :].reshape(cells)
+    outer += jnp.where(beside, rotor, 0.0)
+    finished(sums, inner_ref[...] - outer, basis_ref, next_ref, hess_ref)
 
 
 def one_exchange(near, beyond, far, panel_inverse, basis, jac_block, face_coef, rotor_offset):
@@ -373,7 +380,6 @@
         early_kernel,
         out_shape=(
             pltpu.VMEM((1, width), jnp.float32),
-            pltpu.VMEM((1, width), jnp.float32),
             pltpu.VMEM((ncomp, ncomp, width), jnp.float32),
             pltpu.VMEM(basis.shape, basis.dtype),
             pltpu.VMEM(face_coef.shape, face_coef.dtype),
@@ -381,7 +387,7 @@
             pltpu.SMEM(rotor_offset.shape, rotor_offset.dtype),
         ),
         in_specs=[anywhere] * 5,
-        out_specs=specs(6) + specs(0, 1),
+        out_specs=specs(5) + specs(0, 1),
         scratch_shapes=[pltpu.VMEM(jac_block.shape, jac_block.dtype), pltpu.SemaphoreType.DMA((5,))],
         name="early",
     )(basis, jac_block, face_coef, panel_inverse, rotor_offset)
@@ -392,7 +398,7 @@
             pltpu.VMEM((ncomp, width), jnp.float32),
             pltpu.VMEM((ncomp, width), jnp.float32),
         ),
-        in_specs=specs(10),
+        in_specs=specs(9),
         out_specs=specs(3),
         name="local",
     )(*in_vmem(near, beyond, *far, panel_inverse, basis, face_coef, *early))

time: 27.5 us -> 26.7 us (0.971)
  blocking collectives: 15.8 us -> 15.1 us
    all_to_all x1, blocking collectives: 15.8 us -> 15.1 us  [exchanged(): return lax.all_to_all(slots, AXES, 0, 0, tiled=True).reshape(rows.shape)]
where the time goes in v8:
time: 26.7 us; the launch traced here: 26.5 us
  blocking collectives  15.1 us (57%)
  starting transfers between devices  7 us (26%)
  Pallas kernels  3.04 us (11%)
  between operations  1.34 us (5%)
    all_to_all x1, blocking collectives, exchanged(): return lax.all_to_all(slots, AXES, 0, 0, tiled=True).reshape(rows.shape)  15.1 us
    ppermute x1, starting transfers between devices, on_device(): beyond = lax.ppermute(basis, 'theta', turned)  3.82 us
    ppermute x1, starting transfers between devices, on_device(): far = [far_basis, lax.ppermute(face_coef, 'band', pairs)]  3.03 us
    pallas_call x1, Pallas kernels, one_exchange(): pl.pallas_call(early_kernel, out_shape=(pltpu.VMEM((1, width), jnp.float3...  1.25 us
    pallas_call x1, Pallas kernels, one_exchange(): pl.pallas_call(lambda *refs: merged_kernel(theta_count, band_count, *refs...  1.05 us
    pallas_call x1, Pallas kernels, one_exchange(): pl.pallas_call(local_kernel, out_shape=(pltpu.VMEM((devices * message_row...  0.74 us
  transfers between devices with their start and end apart: 4, of which 0 were waited for; matrix products, arithmetic and copies ran while one was open for 0% of the time, Pallas kernels for 5%

profile of v8, /device:TPU:0, one launch (start us, length us, event | category | flops | bytes accessed | tf_op | source)
XLA Modules:
  0.0 26.5 jit_solution(14413155784931554443)
XLA Ops:
  0.6 3.0 %collective-permute-start.3 = (f32[4,5,1,128]{3,2,1,0:T(1,128)}, f32[4,5,1,128]{3,2,1,0:T(1,128)S(1)}, u32[]{:S(2)}, u32[]{:S(2)}) collective-permute-start(f32[4,5,1,128]{3,2,1,0:T(1,128)} %face_hbm.1), channel_id=1, source_target_pairs={{0,1},{1,0},{2,3},{3,2},{4,5},{5,4},{6,7},{7,6},{8,9},{9,8},{10,11... | collective-permute-start | bytes 30728 | tf_op jit(solution)/shard_map/ppermute | solution.py:437
  3.7 0.0 collective-permute-start
  3.7 0.2 collective-permute-start.2
  3.8 3.8 %collective-permute-start.1 = (f32[4,5,1,128]{3,2,1,0:T(1,128)}, f32[4,5,1,128]{3,2,1,0:T(1,128)S(1)}, u32[]{:S(2)}, u32[]{:S(2)}) collective-permute-start(f32[4,5,1,128]{3,2,1,0:T(1,128)} %basis_hbm.1), channel_id=1, source_target_pairs={{0,28},{4,8},{8,4},{12,16},{16,12},{20,24},{24,20},{28,0},{1,29},{... | collective-permute-start | bytes 30728 | tf_op jit(solution)/shard_map/ppermute | solution.py:440
  8.3 1.2 %early.1 = (f32[1,128]{1,0:T(1,128)S(1)}, f32[5,5,128]{2,1,0:T(8,128)S(1)}, f32[4,5,1,128]{3,2,1,0:T(1,128)S(1)}, f32[4,5,1,128]{3,2,1,0:T(1,128)S(1)}, bf16[1,2...) custom-call(f32[4,5,1,128]{3,2,1,0:T(1,128)} %basis_hbm.1, f32[5,5,1,128]{3,2,1,0:T(1,128)} %jac_hbm.1, ...), custom_call_target="tpu_custom_call" | custom-call | tf_op jit(solution)/shard_map/early/pallas_call | solution.py:379
  9.5 0.0 collective-permute-done.3.far_face_ref
  9.6 0.0 collective-permute-done.near_ref
  9.6 0.0 collective-permute-done.2.far_basis_ref
  9.6 0.0 collective-permute-done.1.beyond_ref
  9.6 0.7 %local.1 = (bf16[832,128]{1,0:T(8,128)(2,1)S(1)}, f32[5,128]{1,0:T(8,128)S(1)}, f32[5,128]{1,0:T(8,128)S(1)}) custom-call(f32[4,5,1,128]{3,2,1,0:T(1,128)S(1)} %collective-permute-done.near_ref, f32[4,5,1,128]{3,2,1,0:T(1,128)S(1)} %collective-permute-done.1.beyond_ref, f32[4,5,1,128]{3,2,1,0:T(1,128)S(1)} %collective-permute-done.2.far_basis_ref, ...), custom_call_target="tpu_custom_call" | custom-call | tf_op jit(solution)/shard_map/local/pallas_call | solution.py:394
  10.3 15.1 %all_to_all.5 = bf16[32,13,2,128]{3,2,1,0:T(2,128)(2,1)S(1)} all-to-all(bf16[32,13,2,128]{3,2,1,0:T(2,128)(2,1)S(1)} %bitcast.4), channel_id=1, replica_groups=mesh['theta'=8,'band'=4] {'theta','band'}, dimensions={0} | all-to-all | bytes 425984 | tf_op jit(solution)/shard_map/all_to_all | solution.py:423
  25.4 1.0 %merged.1 = (f32[5,1,128]{2,1,0:T(1,128)}, f32[5,1,128]{2,1,0:T(1,128)}, f32[1,5]{1,0:T(1,128)}) custom-call(s32[1]{0:T(128)S(4)} %get-tuple-element.15.refs_0_, f32[832,128]{1,0:T(8,128)S(1)} %convert.1.refs_1_, f32[5,128]{1,0:T(8,128)S(1)} %get-tuple-element.22.refs_2_, f32[5,128]{1,0:T(8,128)S(1)} %get-tuple-element.23.refs_3_, ...), custom_call_target="tpu_custom_call" | custom-call | tf_op jit(solution)/shard_map/merged/pallas_call | solution.py:407
  (1 shorter events, 0.0 us)
Async XLA Ops:
  0.6 8.9 %collective-permute-start.3 = (f32[4,5,1,128]{3,2,1,0:T(1,128)}, f32[4,5,1,128]{3,2,1,0:T(1,128)S(1)}, u32[]{:S(2)}, u32[]{:S(2)}) collective-permute-start(f32[4,5,1,128]{3,2,1,0:T(1,128)} %face_hbm.1), channel_id=1, source_target_pairs={{0,1},{1,0},{2,3},{3,2},{4,5},{5,4},{6,7},{7,6},{8,9},{9,8},{10,11... | collective-permute-start | bytes 30728 | tf_op jit(solution)/shard_map/ppermute | solution.py:437
  3.7 5.9 %collective-permute-start = (f32[4,5,1,128]{3,2,1,0:T(1,128)}, f32[4,5,1,128]{3,2,1,0:T(1,128)S(1)}, u32[]{:S(2)}, u32[]{:S(2)}) collective-permute-start(f32[4,5,1,128]{3,2,1,0:T(1,128)} %basis_hbm.1), channel_id=1, source_target_pairs={{0,4},{4,0},{8,12},{12,8},{16,20},{20,16},{24,28},{28,24},{1,5},{5... | collective-permute-start | bytes 30728 | tf_op jit(solution)/shard_map/ppermute | solution.py:438
  3.7 5.9 %collective-permute-start.2 = (f32[4,5,1,128]{3,2,1,0:T(1,128)}, f32[4,5,1,128]{3,2,1,0:T(1,128)S(1)}, u32[]{:S(2)}, u32[]{:S(2)}) collective-permute-start(f32[4,5,1,128]{3,2,1,0:T(1,128)} %basis_hbm.1), channel_id=1, source_target_pairs={{0,1},{1,0},{2,3},{3,2},{4,5},{5,4},{6,7},{7,6},{8,9},{9,8},{10,11... | collective-permute-start | bytes 30728 | tf_op jit(solution)/shard_map/ppermute | solution.py:436
  3.8 5.8 %collective-permute-start.1 = (f32[4,5,1,128]{3,2,1,0:T(1,128)}, f32[4,5,1,128]{3,2,1,0:T(1,128)S(1)}, u32[]{:S(2)}, u32[]{:S(2)}) collective-permute-start(f32[4,5,1,128]{3,2,1,0:T(1,128)} %basis_hbm.1), channel_id=1, source_target_pairs={{0,28},{4,8},{8,4},{12,16},{16,12},{20,24},{24,20},{28,0},{1,29},{... | collective-permute-start | bytes 30728 | tf_op jit(solution)/shard_map/ppermute | solution.py:440
